TPU v7x, 32 devices: a whole 2x2x4 slice. The times are simulated.
32 devices in a mesh: dp: 4 (over y, x), expert: 8 (over z, core).
Axes of the slice: x: 2, y: 2, z: 4, core: 2. Of those that a mesh axis runs over, the one named last changes fastest.
Arguments:
- tokens: bfloat16 [4096, 1024], P(('dp', 'expert')), may hold values from -6 to 6
- expert_ids: int32 [4096, 4], P(('dp', 'expert')), may hold values from 0 to 7, all different within a row; in each aligned block of 128 rows (0 to 127, 128 to 255, ...) at most 96 rows name the same one
- gate_probs: float32 [4096, 4], P(('dp', 'expert')), may hold values from 0.05 to 0.6
- w_gate: bfloat16 [8, 1024, 512], P('expert', 'dp'), may hold values from -0.1875 to 0.1875
- w_up: bfloat16 [8, 1024, 512], P('expert', 'dp'), may hold values from -0.1875 to 0.1875
- w_down: bfloat16 [8, 512, 1024], P('expert', 'dp'), may hold values from -0.25 to 0.25
- cotangent: bfloat16 [4096, 1024], P(('dp', 'expert')), may hold values from -6 to 6
Outputs:
- mixed: bfloat16 [4096, 1024], P(('dp', 'expert'))
- input_grad: bfloat16 [4096, 1024], P(('dp', 'expert'))
- prob_grad: float32 [4096, 4], P(('dp', 'expert'))
- gate_grad: bfloat16 [8, 1024, 512], P('expert', 'dp')
- up_grad: bfloat16 [8, 1024, 512], P('expert', 'dp')
- down_grad: bfloat16 [8, 512, 1024], P('expert', 'dp')
Inputs may be any that keep to these rules, and one draw needn't show every extreme that they name: `expert_ids`: each row names 4 different experts. Among the rows of one device no expert is named more than 96 times, and in every draw some expert is named exactly 96 times by the rows of some device.
All inputs are finite; a program needn't handle non-finite values.
Results may differ from a plain program's by a relative error of at most 0.015.
Values may be sent and summed in bfloat16 or wider, within the bound.
No kernel may reach another device: no remote copies, remote signals or barrier semaphores. Data moves between devices by JAX's collectives and lax.ppermute only.
A program may use at most 64 MiB of HBM per device.

v0:
```python
import jax
import jax.numpy as jnp
from jax import lax
from jax.sharding import PartitionSpec as P


def per_device(tokens, expert_ids, gate_probs, w_gate, w_up, w_down, cotangent):
    tok_dev = tokens.shape[0]
    model_width = tokens.shape[1]
    top_count = expert_ids.shape[1]
    hidden_width = w_gate.shape[2]
    expert_devices = lax.axis_size("expert")
    data_devices = lax.axis_size("dp")
    exp_dev = w_gate.shape[0]
    experts = exp_dev * expert_devices
    pair_count = tok_dev * top_count
    capacity = min(tok_dev, 3 * tok_dev * top_count // (2 * experts))
    grad_scale = (experts / (tok_dev * top_count * data_devices * expert_devices)) ** 0.5
    flat_ids = expert_ids.reshape(pair_count)
    onehot = (flat_ids[:, None] == jnp.arange(experts, dtype=jnp.int32)[None, :]).astype(jnp.int32)
    slot_rank = jnp.sum((jnp.cumsum(onehot, axis=0) - 1) * onehot, axis=1)
    target = flat_ids * capacity + slot_rank
    slot_owner = (
        jnp.full((experts * capacity,), pair_count, jnp.int32)
        .at[target]
        .set(jnp.arange(pair_count, dtype=jnp.int32))
    )
    token_rows = jnp.where(slot_owner < pair_count, slot_owner // top_count, tok_dev)
    padded_tokens = jnp.concatenate([tokens, jnp.zeros((1, model_width), tokens.dtype)], axis=0)
    send_rows = padded_tokens[token_rows].reshape(experts, capacity, model_width)
    out_pairs = (gate_probs[:, :, None] * cotangent.astype(jnp.float32)[:, None, :]).astype(
        jnp.bfloat16
    )
    out_pairs = jnp.concatenate(
        [out_pairs.reshape(pair_count, model_width), jnp.zeros((1, model_width), jnp.bfloat16)],
        axis=0,
    )
    send_grads = out_pairs[slot_owner].reshape(experts, capacity, model_width)
    full_gate, full_up, full_down = (
        lax.all_gather(w_gate, "dp", axis=1, tiled=True),
        lax.all_gather(w_up, "dp", axis=1, tiled=True),
        lax.all_gather(w_down, "dp", axis=1, tiled=True),
    )
    received = lax.all_to_all(send_rows, "expert", split_axis=0, concat_axis=0, tiled=True)
    item_count = received.shape[1]
    grouped = received.reshape(expert_devices, exp_dev, item_count, model_width)
    gate_pre = jnp.einsum("sacd,adf->sacf", grouped, full_gate, preferred_element_type=jnp.float32)
    up_pre = jnp.einsum("sacd,adf->sacf", grouped, full_up, preferred_element_type=jnp.float32)
    hidden = (jax.nn.silu(gate_pre) * up_pre).astype(jnp.bfloat16)
    result = jnp.einsum("sacf,afd->sacd", hidden, full_down, preferred_element_type=jnp.float32)
    result = result.astype(jnp.bfloat16).reshape(experts, item_count, model_width)
    gate_pre, up_pre, hidden, result = (
        gate_pre.reshape(experts, item_count, hidden_width),
        up_pre.reshape(experts, item_count, hidden_width),
        hidden.reshape(experts, item_count, hidden_width),
        result,
    )
    returned = lax.all_to_all(result, "expert", split_axis=0, concat_axis=0, tiled=True)
    returned, kept_rows, gate_pre, up_pre, hidden = (returned, received, gate_pre, up_pre, hidden)
    recv_grads = lax.all_to_all(send_grads, "expert", split_axis=0, concat_axis=0, tiled=True)
    back_gate, back_up, back_down = (
        lax.all_gather(w_gate, "dp", axis=1, tiled=True),
        lax.all_gather(w_up, "dp", axis=1, tiled=True),
        lax.all_gather(w_down, "dp", axis=1, tiled=True),
    )
    grouped_grads = recv_grads.reshape(expert_devices, exp_dev, capacity, model_width)
    grouped_hidden = hidden.reshape(expert_devices, exp_dev, capacity, hidden_width)
    grouped_rows = kept_rows.reshape(expert_devices, exp_dev, capacity, model_width)
    gate_wide = gate_pre.reshape(expert_devices, exp_dev, capacity, hidden_width)
    up_wide = up_pre.reshape(expert_devices, exp_dev, capacity, hidden_width)
    down_part = (
        jnp.einsum(
            "sacf,sacd->afd", grouped_hidden, grouped_grads, preferred_element_type=jnp.float32
        )
        * grad_scale
    )
    hidden_grad = jnp.einsum(
        "sacd,afd->sacf", grouped_grads, back_down, preferred_element_type=jnp.float32
    )
    sigmoid_gate = jax.nn.sigmoid(gate_wide)
    up_grad_pre = (hidden_grad * jax.nn.silu(gate_wide)).astype(jnp.bfloat16)
    gate_grad_pre = (
        hidden_grad * up_wide * sigmoid_gate * (1.0 + gate_wide * (1.0 - sigmoid_gate))
    ).astype(jnp.bfloat16)
    row_grad = jnp.einsum(
        "sacf,adf->sacd", gate_grad_pre, back_gate, preferred_element_type=jnp.float32
    ) + jnp.einsum("sacf,adf->sacd", up_grad_pre, back_up, preferred_element_type=jnp.float32)
    row_grad = row_grad.astype(jnp.bfloat16).reshape(experts, capacity, model_width)
    back_grads = lax.all_to_all(row_grad, "expert", split_axis=0, concat_axis=0, tiled=True)
    gate_part = (
        jnp.einsum(
            "sacd,sacf->adf", grouped_rows, gate_grad_pre, preferred_element_type=jnp.float32
        )
        * grad_scale
    )
    up_part = (
        jnp.einsum("sacd,sacf->adf", grouped_rows, up_grad_pre, preferred_element_type=jnp.float32)
        * grad_scale
    )
    gate_sum, up_sum, down_sum = (
        lax.psum_scatter(
            gate_part.astype(jnp.bfloat16), "dp", scatter_dimension=1, tiled=True
        ).astype(jnp.float32),
        lax.psum_scatter(
            up_part.astype(jnp.bfloat16), "dp", scatter_dimension=1, tiled=True
        ).astype(jnp.float32),
        lax.psum_scatter(
            down_part.astype(jnp.bfloat16), "dp", scatter_dimension=1, tiled=True
        ).astype(jnp.float32),
    )
    pair_out = returned.reshape(experts * capacity, model_width)[target].reshape(
        tok_dev, top_count, model_width
    )
    mixed = jnp.sum(gate_probs[:, :, None] * pair_out.astype(jnp.float32), axis=1).astype(
        jnp.bfloat16
    )
    prob_grad = jnp.einsum("td,tkd->tk", cotangent, pair_out, preferred_element_type=jnp.float32)
    pair_grads = back_grads.reshape(experts * capacity, model_width)[target].reshape(
        tok_dev, top_count, model_width
    )
    input_grad = jnp.sum(pair_grads.astype(jnp.float32), axis=1).astype(jnp.bfloat16)
    return (
        mixed,
        input_grad,
        prob_grad,
        gate_sum.astype(jnp.bfloat16),
        up_sum.astype(jnp.bfloat16),
        down_sum.astype(jnp.bfloat16),
    )


def solution(mesh):
    return jax.shard_map(
        per_device,
        mesh=mesh,
        in_specs=(
            P(("dp", "expert"), None),
            P(("dp", "expert"), None),
            P(("dp", "expert"), None),
            P("expert", "dp", None),
            P("expert", "dp", None),
            P("expert", "dp", None),
            P(("dp", "expert"), None),
        ),
        out_specs=(
            P(("dp", "expert"), None),
            P(("dp", "expert"), None),
            P(("dp", "expert"), None),
            P("expert", "dp", None),
            P("expert", "dp", None),
            P("expert", "dp", None),
        ),
        check_vma=False,
    )
```

profile of v0, /device:TPU:0, one launch (start us, length us, event | category | flops | bytes accessed | tf_op | source)
XLA Modules:
  0.0 220.2 jit_solution(7961308410853271178)
XLA Ops:
  7.2 0.7 broadcast_multiply_fusion
  7.8 0.8 copy.16
  8.6 0.1 eq.29
  8.7 0.1 eq.25
  8.9 0.1 copy.15
  9.0 0.1 mul.86
  9.1 1.1 reduce-window.6
  10.2 0.2 slice_reduce_fusion
  10.5 0.1 fusion.31
  10.6 2.4 %scatter_custom_fusion = s32[768]{0:T(1024)S(1)} fusion(s32[512]{0:T(512)S(1)} %bitcast.136, s32[512]{0:T(512)S(1)} %iota.11, s32[]{:T(128)} %constant.16.clone.1), kind=kCustom, calls=%fused_computation.69 | custom fusion | bytes 3076 | tf_op jit(solution)/shard_map/scatter | solution.py:26
  13.1 1.0 concatenate.6
  14.1 3.6 %gather_fusion = bf16[768,1024]{1,0:T(8,128)(2,1)} fusion(bf16[129,1024]{1,0:T(8,128)(2,1)S(1)} %concatenate.6, s32[1024]{0:T(1024)S(1)} %get-tuple-element.12), kind=kCustom, calls=%fused_computation | custom fusion | bytes 3148800 | tf_op jit(solution)/shard_map/gather | solution.py:30
  17.6 6.5 %all-to-all-start = ((bf16[8,96,1024]{2,1,0:T(8,128)(2,1)}), bf16[8,96,1024]{2,1,0:T(8,128)(2,1)}, u32[]{:S(2)}, u32[]{:S(2)}) async-start(bf16[8,96,1024]{2,1,0:T(8,128)(2,1)} %bitcast.4), calls=%async_computation | async-start | bytes 3145728 | tf_op jit(solution)/shard_map/all_to_all | solution.py:44
  24.1 0.0 all-gather.6.cloned.1.call-start
  24.2 0.7 all-gather.6.cloned.1.call-update
  24.8 0.0 all-gather.8.cloned.1.call-start
  24.9 0.7 all-gather.8.cloned.1.call-update
  25.6 0.1 copy.14
  25.7 0.1 mul.91
  25.8 0.0 copy-done.5
  25.8 1.9 mul.93
  27.7 2.0 mul.94
  29.7 0.2 multiply_convert_fusion
  29.9 0.1 concatenate.7
  30.0 3.6 %gather_fusion.2 = bf16[768,1024]{1,0:T(8,128)(2,1)} fusion(bf16[513,1024]{1,0:T(8,128)(2,1)S(1)} %concatenate.7, s32[1024]{0:T(1024)S(1)} %get-tuple-element.11), kind=kCustom, calls=%fused_computation.2 | custom fusion | bytes 3148800 | tf_op jit(solution)/shard_map/gather | solution.py:38
  33.6 28.4 %all-to-all-done = bf16[8,96,1024]{2,1,0:T(8,128)(2,1)} async-done(((bf16[8,96,1024]{2,1,0:T(8,128)(2,1)}), bf16[8,96,1024]{2,1,0:T(8,128)(2,1)}, u32[]{:S(2)}, u32[]{:S(2)}) %all-to-all-start) | async-done | bytes 1572896 | tf_op jit(solution)/shard_map/all_to_all | solution.py:44
  62.0 3.6 %all-to-all-start.2 = ((bf16[8,96,1024]{2,1,0:T(8,128)(2,1)}), bf16[8,96,1024]{2,1,0:T(8,128)(2,1)S(1)}, u32[]{:S(2)}, u32[]{:S(2)}) async-start(bf16[8,96,1024]{2,1,0:T(8,128)(2,1)} %bitcast.21), calls=%async_computation.2 | async-start | bytes 3145728 | tf_op jit(solution)/shard_map/all_to_all | solution.py:60
  65.6 0.0 all-gather.4.cloned.1.call-start
  65.7 0.7 all-gather.4.cloned.1.call-update
  66.4 0.0 reduce-scatter.8.cloned.1.call-start
  66.4 0.0 all-gather.6.cloned.1.call-done
  66.4 3.8 %fusion.19 = f32[8,96,512]{2,1,0:T(8,128)} fusion(bf16[8,96,1024]{2,1,0:T(8,128)(2,1)} %all-to-all-done, bf16[1,1024,512]{2,1,0:T(8,128)(2,1)} %all-gather.6.cloned.1.call-done), kind=kOutput, calls=%fused_computation.37 | convolution fusion | flops 805306368 | bytes 4194304 | tf_op jit(solution)/shard_map/sacd,adf->sacf/dot_general | solution.py:48
  70.2 12.9 %all-gather.8.cloned.1.call-done = bf16[1,512,1024]{2,1,0:T(8,128)(2,1)} async-done(((bf16[1,128,1024]{2,1,0:T(8,128)(2,1)}), bf16[1,512,1024]{2,1,0:T(8,128)(2,1)}) %all-gather.8.cloned.1.call-update) | async-done | bytes 1048592 | tf_op jit(solution)/shard_map/all_gather | solution.py:42
  83.1 20.2 %all-to-all-done.2 = bf16[8,96,1024]{2,1,0:T(8,128)(2,1)S(1)} async-done(((bf16[8,96,1024]{2,1,0:T(8,128)(2,1)}), bf16[8,96,1024]{2,1,0:T(8,128)(2,1)S(1)}, u32[]{:S(2)}, u32[]{:S(2)}) %all-to-all-start.2) | async-done | bytes 1572896 | tf_op jit(solution)/shard_map/all_to_all | solution.py:60
  103.3 3.4 %fusion.15 = f32[8,96,512]{2,1,0:T(8,128)} fusion(bf16[8,96,1024]{2,1,0:T(8,128)(2,1)S(1)} %all-to-all-done.2, bf16[1,512,1024]{2,1,0:T(8,128)(2,1)} %all-gather.8.cloned.1.call-done), kind=kOutput, calls=%fused_computation.33 | convolution fusion | flops 805306368 | bytes 4194304 | tf_op jit(solution)/shard_map/sacd,afd->sacf/dot_general | solution.py:77
  106.7 4.8 %all-gather.4.cloned.1.call-done = bf16[1,1024,512]{2,1,0:T(8,128)(2,1)} async-done(((bf16[1,256,512]{2,1,0:T(8,128)(2,1)}), bf16[1,1024,512]{2,1,0:T(8,128)(2,1)}) %all-gather.4.cloned.1.call-update) | async-done | bytes 1048592 | tf_op jit(solution)/shard_map/all_gather | solution.py:40
  111.5 5.2 %fusion.26 = (bf16[8,96,512]{2,1,0:T(8,128)(2,1)S(1)}, bf16[8,1,96,512]{3,2,0,1:T(8,128)(2,1)}, bf16[8,96,512]{2,1,0:T(8,128)(2,1)S(1)}) fusion(f32[8,96,512]{2,1,0:T(8,128)} %fusion.15, f32[8,96,512]{2,1,0:T(8,128)} %fusion.19, bf16[8,96,1024]{2,1,0:T(8,128)(2,1)} %all-to-all-done, bf16[1,1024,512]{2,1,0:T(8,128)(2,1)} %all-gather.4.cloned.1.call-done), kind=kOutput, calls=%fused_computation.44 | convolution fusion | flops 811204608 | bytes 8126464 | tf_op jit(solution)/shard_map/sacd,adf->sacf/dot_general | solution.py:47
  116.8 0.9 copy-done.9
  117.6 2.0 fusion.14
  119.6 0.0 reduce-scatter.8.cloned.1.call-update
  119.7 3.2 %convolution_convert_fusion = bf16[8,96,1024]{2,1,0:T(8,128)(2,1)} fusion(bf16[8,96,512]{2,1,0:T(8,128)(2,1)} %copy-done.9, bf16[1,512,1024]{2,1,0:T(8,128)(2,1)S(1)} %copy-done.8), kind=kOutput, calls=%fused_computation.14 | convolution fusion | flops 806092800 | bytes 3407872 | tf_op jit(solution)/shard_map/sacf,afd->sacd/dot_general | solution.py:50
  122.9 4.6 %all-to-all-start.1 = ((bf16[8,96,1024]{2,1,0:T(8,128)(2,1)}), bf16[8,96,1024]{2,1,0:T(8,128)(2,1)S(1)}, u32[]{:S(2)}, u32[]{:S(2)}) async-start(bf16[8,96,1024]{2,1,0:T(8,128)(2,1)} %convolution_convert_fusion), calls=%async_computation.1 | async-start | bytes 3145728 | tf_op jit(solution)/shard_map/all_to_all | solution.py:58
  127.5 0.0 reduce-scatter.4.cloned.1.call-start
  127.6 3.7 %fusion.12 = bf16[1,1024,512]{2,1,0:T(8,128)(2,1)} fusion(bf16[8,96,1024]{2,1,0:T(8,128)(2,1)} %all-to-all-done, bf16[8,1,96,512]{3,2,0,1:T(8,128)(2,1)} %get-tuple-element.7), kind=kOutput, calls=%fused_computation.30 | convolution fusion | flops 806354944 | bytes 3407872 | tf_op jit(solution)/shard_map/sacd,sacf->adf/dot_general | solution.py:91
  131.3 0.0 reduce-scatter.4.cloned.1.call-update
  131.4 2.3 %fusion.21 = f32[8,96,1024]{2,1,0:T(8,128)S(1)} fusion(bf16[1,1024,512]{2,1,0:T(8,128)(2,1)S(1)} %copy-done.3, bf16[8,1,96,512]{3,2,0,1:T(8,128)(2,1)} %get-tuple-element.7), kind=kOutput, calls=%fused_computation.39 | convolution fusion | flops 805306368 | bytes 4980736 | tf_op jit(solution)/shard_map/sacf,adf->sacd/dot_general | solution.py:85
  133.7 2.2 add_convert_fusion
  135.8 29.5 %all-to-all-done.1 = bf16[8,96,1024]{2,1,0:T(8,128)(2,1)S(1)} async-done(((bf16[8,96,1024]{2,1,0:T(8,128)(2,1)}), bf16[8,96,1024]{2,1,0:T(8,128)(2,1)S(1)}, u32[]{:S(2)}, u32[]{:S(2)}) %all-to-all-start.1) | async-done | bytes 1572896 | tf_op jit(solution)/shard_map/all_to_all | solution.py:58
  165.3 3.6 %all-to-all-start.3 = ((bf16[8,96,1024]{2,1,0:T(8,128)(2,1)}), bf16[8,96,1024]{2,1,0:T(8,128)(2,1)S(1)}, u32[]{:S(2)}, u32[]{:S(2)}) async-start(bf16[8,96,1024]{2,1,0:T(8,128)(2,1)} %add_convert_fusion), calls=%async_computation.3 | async-start | bytes 3145728 | tf_op jit(solution)/shard_map/all_to_all | solution.py:89
  168.9 0.2 reduce-scatter.6.cloned.1.call-start
  169.1 3.6 %fusion.13 = bf16[1,1024,512]{2,1,0:T(8,128)(2,1)} fusion(bf16[8,96,1024]{2,1,0:T(8,128)(2,1)} %all-to-all-done, bf16[8,96,512]{2,1,0:T(8,128)(2,1)} %copy-done.4), kind=kOutput, calls=%fused_computation.31 | convolution fusion | flops 806354944 | bytes 3407872 | tf_op jit(solution)/shard_map/sacd,sacf->adf/dot_general | solution.py:97
  172.8 0.0 reduce-scatter.6.cloned.1.call-update
  172.8 2.8 %gather_fusion.1 = bf16[512,1024]{1,0:T(8,128)(2,1)} fusion(bf16[768,1024]{1,0:T(8,128)(2,1)S(1)} %bitcast.133, s32[1024]{0:T(1024)S(1)} %pad_clamp_fusion.1), kind=kCustom, calls=%fused_computation.1 | custom fusion | bytes 2099200 | tf_op jit(solution)/shard_map/gather | solution.py:111
  175.6 1.5 reshape.149
  177.1 0.0 copy-start
  177.1 0.0 copy-done.6
  177.1 1.1 fusion.29
  178.3 0.0 copy-done
  178.3 0.7 copy.20
  179.0 27.7 %all-to-all-done.3 = bf16[8,96,1024]{2,1,0:T(8,128)(2,1)S(1)} async-done(((bf16[8,96,1024]{2,1,0:T(8,128)(2,1)}), bf16[8,96,1024]{2,1,0:T(8,128)(2,1)S(1)}, u32[]{:S(2)}, u32[]{:S(2)}) %all-to-all-start.3) | async-done | bytes 1572896 | tf_op jit(solution)/shard_map/all_to_all | solution.py:89
  206.6 2.0 gather_fusion.3
  208.7 0.4 reshape.154
  209.1 2.1 reduce_sum.35
  211.2 2.1 multiply_reduce_fusion
  (26 shorter events, 0.1 us)
Async XLA Ops:
  17.6 8.0 %copy-start.7 = (f32[128,4]{0,1:T(4,128)S(1)}, f32[128,4]{0,1:T(4,128)}, u32[]{:S(2)}) copy-start(f32[128,4]{0,1:T(4,128)} %param.9) | copy-start | bytes 6148
  17.6 8.2 %copy-start.5 = (bf16[128,1024]{1,0:T(8,128)(2,1)S(1)}, bf16[128,1024]{1,0:T(8,128)(2,1)}, u32[]{:S(2)}) copy-start(bf16[128,1024]{1,0:T(8,128)(2,1)} %param.13) | copy-start | bytes 786436
  17.6 44.4 %all-to-all-start = ((bf16[8,96,1024]{2,1,0:T(8,128)(2,1)}), bf16[8,96,1024]{2,1,0:T(8,128)(2,1)}, u32[]{:S(2)}, u32[]{:S(2)}) async-start(bf16[8,96,1024]{2,1,0:T(8,128)(2,1)} %bitcast.4), calls=%async_computation | async-start | bytes 3145728 | tf_op jit(solution)/shard_map/all_to_all | solution.py:44
  24.1 42.3 %all-gather.6.cloned.1.call-start = ((), (), s32[]{:S(2)}) async-start(), calls=%async_computation.8 | async-start | bytes 1310720 | tf_op jit(solution)/shard_map/all_gather | solution.py:41
  24.8 58.3 %all-gather.8.cloned.1.call-start = ((), (), s32[]{:S(2)}) async-start(), calls=%async_computation.9 | async-start | bytes 1310720 | tf_op jit(solution)/shard_map/all_gather | solution.py:42
  62.0 41.3 %all-to-all-start.2 = ((bf16[8,96,1024]{2,1,0:T(8,128)(2,1)}), bf16[8,96,1024]{2,1,0:T(8,128)(2,1)S(1)}, u32[]{:S(2)}, u32[]{:S(2)}) async-start(bf16[8,96,1024]{2,1,0:T(8,128)(2,1)} %bitcast.21), calls=%async_computation.2 | async-start | bytes 3145728 | tf_op jit(solution)/shard_map/all_to_all | solution.py:60
  65.6 45.9 %all-gather.4.cloned.1.call-start = ((), (), s32[]{:S(2)}) async-start(), calls=%async_computation.7 | async-start | bytes 1310720 | tf_op jit(solution)/shard_map/all_gather | solution.py:40
  66.4 147.0 %reduce-scatter.8.cloned.1.call-start = ((), (), s32[]{:S(2)}) async-start(), calls=%async_computation.12 | async-start | bytes 1310720 | tf_op jit(solution)/shard_map/reduce_scatter | solution.py:107
  116.7 0.9 copy-start.9
  116.8 16.9 %copy-start.4 = (bf16[8,96,512]{2,1,0:T(8,128)(2,1)}, bf16[8,96,512]{2,1,0:T(8,128)(2,1)S(1)}, u32[]{:S(2)}) copy-start(bf16[8,96,512]{2,1,0:T(8,128)(2,1)S(1)} %get-tuple-element.6) | copy-start | bytes 2359300
  117.6 2.0 copy-start.8
  122.9 42.4 %all-to-all-start.1 = ((bf16[8,96,1024]{2,1,0:T(8,128)(2,1)}), bf16[8,96,1024]{2,1,0:T(8,128)(2,1)S(1)}, u32[]{:S(2)}, u32[]{:S(2)}) async-start(bf16[8,96,1024]{2,1,0:T(8,128)(2,1)} %convolution_convert_fusion), calls=%async_computation.1 | async-start | bytes 3145728 | tf_op jit(solution)/shard_map/all_to_all | solution.py:58
  127.5 85.9 %reduce-scatter.4.cloned.1.call-start = ((), (), s32[]{:S(2)}) async-start(), calls=%async_computation.10 | async-start | bytes 1310720 | tf_op jit(solution)/shard_map/reduce_scatter | solution.py:101
  127.6 3.8 %copy-start.3 = (bf16[1,1024,512]{2,1,0:T(8,128)(2,1)S(1)}, bf16[1,1024,512]{2,1,0:T(8,128)(2,1)}, u32[]{:S(2)}) copy-start(bf16[1,1024,512]{2,1,0:T(8,128)(2,1)} %all-gather.4.cloned.1.call-done) | copy-start | bytes 3145732
  131.3 2.3 %copy-start.2 = (bf16[1,1024,512]{2,1,0:T(8,128)(2,1)S(1)}, bf16[1,1024,512]{2,1,0:T(8,128)(2,1)}, u32[]{:S(2)}) copy-start(bf16[1,1024,512]{2,1,0:T(8,128)(2,1)} %all-gather.6.cloned.1.call-done) | copy-start | bytes 3145732
  165.3 41.3 %all-to-all-start.3 = ((bf16[8,96,1024]{2,1,0:T(8,128)(2,1)}), bf16[8,96,1024]{2,1,0:T(8,128)(2,1)S(1)}, u32[]{:S(2)}, u32[]{:S(2)}) async-start(bf16[8,96,1024]{2,1,0:T(8,128)(2,1)} %add_convert_fusion), calls=%async_computation.3 | async-start | bytes 3145728 | tf_op jit(solution)/shard_map/all_to_all | solution.py:89
  168.9 44.5 %reduce-scatter.6.cloned.1.call-start = ((), (), s32[]{:S(2)}) async-start(), calls=%async_computation.11 | async-start | bytes 1310720 | tf_op jit(solution)/shard_map/reduce_scatter | solution.py:104
  175.6 1.5 copy-start.6
  177.1 1.2 copy-start
  208.7 2.6 %copy-start.1 = (bf16[128,4,1024]{2,1,0:T(4,128)(2,1)S(1)}, bf16[128,4,1024]{2,1,0:T(4,128)(2,1)}, u32[]{:S(2)}) copy-start(bf16[128,4,1024]{2,1,0:T(4,128)(2,1)} %copy-done) | copy-start | bytes 3145732
Sparse Core Ops, SparseCore 0:
  26.8 27.9 all-gather.5
  56.6 26.4 all-gather.7
  85.0 26.4 all-gather.3
  119.8 27.9 reduce-scatter.7
  151.0 27.9 reduce-scatter.3
  182.3 27.9 reduce-scatter.5
where the time goes:
time: 221 us; the launch traced here: 220 us
  waiting for transfers between devices  126 us (57%)
  matrix products  30.6 us (14%)
  local copies, waits for them, and re-layouts  24.5 us (11%)
  starting transfers between devices  18.7 us (8%)
  between operations  14.4 us (7%)
  other arithmetic  6.42 us (3%)
    all_to_all x1, waiting for transfers between devices, per_device(): lax.all_to_all(result, 'expert', split_axis=0, concat_axis=0, tiled=True)  29.5 us
    all_to_all x1, waiting for transfers between devices, per_device(): lax.all_to_all(send_rows, 'expert', split_axis=0, concat_axis=0, tiled=True)  28.4 us
    all_to_all x1, waiting for transfers between devices, per_device(): lax.all_to_all(row_grad, 'expert', split_axis=0, concat_axis=0, tiled=True)  27.7 us
    all_to_all x1, waiting for transfers between devices, per_device(): lax.all_to_all(send_grads, 'expert', split_axis=0, concat_axis=0, tiled=T...  20.2 us
    all_gather x1, waiting for transfers between devices, per_device(): lax.all_gather(w_down, 'dp', axis=1, tiled=True)  12.9 us
    all_to_all x1, starting transfers between devices, per_device(): lax.all_to_all(send_rows, 'expert', split_axis=0, concat_axis=0, tiled=True)  6.49 us
    dot_general x1, matrix products, per_device(): jnp.einsum('sacd,adf->sacf', grouped, full_gate, preferred_element_type=j...  5.25 us
    all_gather x1, waiting for transfers between devices, per_device(): lax.all_gather(w_gate, 'dp', axis=1, tiled=True)  4.77 us
  transfers between devices with their start and end apart: 10, of which 6 were waited for; matrix products, arithmetic and copies ran while one was open for 20% of the time, Pallas kernels for 0%

commit v1 on v0

v1 whole, which is shorter than its diff:
```python
import jax
import jax.numpy as jnp
from jax import lax
from jax.sharding import PartitionSpec as P

BF = jnp.bfloat16
F32 = jnp.float32


def send(x, axis, flip, only=None):
    size = lax.axis_size(axis)
    pairs = [(j, j ^ flip) for j in range(size) if only is None or only(j, j ^ flip)]
    return lax.ppermute(x, axis, pairs)


def spread(block):
    pairs = lax.axis_size("expert") // 2
    if pairs == 4:
        inner = lambda a, b: a // 2 in (1, 2)
        two = send(block, "expert", 4)
        one = send(block, "expert", 2)
        mid = send(block, "expert", 6, inner)
        far = send(two, "expert", 2, lambda a, b: a // 2 in (1, 2))
        row = lax.axis_index("expert") // 2
        three = jnp.where((row == 1) | (row == 2), mid, far)
        mine = [block, one, two, three]
    else:
        mine = [block] + [send(block, "expert", 2 * m) for m in range(1, pairs)]
    mine = lax.optimization_barrier(jnp.concatenate(mine, axis=0))
    return mine, send(mine, "expert", 1)


def collect(mine, other, rows):
    pairs = lax.axis_size("expert") // 2
    got = send(other, "expert", 1)
    total = (mine.astype(F32) + got.astype(F32)).astype(BF)
    total = lax.optimization_barrier(total)
    parts = [total[m * rows : (m + 1) * rows] for m in range(pairs)]
    out = parts[0].astype(F32)
    for m in range(1, pairs):
        out = out + send(parts[m], "expert", 2 * m).astype(F32)
    return out.astype(BF)


def in_order(parts, own):
    parts = list(parts)
    step = 1
    while step < len(parts):
        odd = (own & step) != 0
        parts = [jnp.where(odd, parts[j ^ step], parts[j]) for j in range(len(parts))]
        step *= 2
    return parts


def gather_rows(shard):
    size = lax.axis_size("dp")
    if size > 8:
        full = lax.all_gather(shard, "dp", axis=0, tiled=False)
        own = lax.axis_index("dp")
        return [lax.dynamic_index_in_dim(full, own ^ m, 0, False) for m in range(size)]
    parts = [shard]
    for m in range(1, size if size != 4 else 3):
        parts.append(send(shard, "dp", m))
    if size == 4:
        half = shard.shape[0] // 2
        lo = send(parts[2][:half], "dp", 1)
        hi = send(parts[1][half:], "dp", 2)
        parts.append(jnp.concatenate([lo, hi], axis=0))
    return parts


def scatter_rows(parts):
    size = lax.axis_size("dp")
    if size > 8:
        whole = jnp.concatenate(in_order(parts, lax.axis_index("dp")))
        return lax.psum_scatter(whole, "dp", scatter_dimension=0, tiled=True)
    total = parts[0].astype(F32)
    for m in range(1, size):
        total = total + send(parts[m], "dp", m).astype(F32)
    return total.astype(BF)


def mm(a, b, dims):
    return lax.dot_general(a, b, ((dims[0], dims[1]), ((), ())), preferred_element_type=F32)


def per_device(tokens, expert_ids, gate_probs, w_gate, w_up, w_down, cotangent):
    rows, width = tokens.shape
    top = expert_ids.shape[1]
    hid = w_gate.shape[2]
    expert_devices = lax.axis_size("expert")
    data_devices = lax.axis_size("dp")
    pairs = expert_devices // 2
    experts = expert_devices
    assert w_gate.shape[0] == 1
    scale = (experts / (rows * top * data_devices * expert_devices)) ** 0.5
    me = lax.axis_index("expert")
    own = lax.axis_index("dp")
    dwidth = width // data_devices
    dhid = hid // data_devices

    def shuffle(x):
        cols = [x[:, j * dwidth : (j + 1) * dwidth] for j in range(data_devices)]
        return jnp.concatenate(in_order(cols, own), axis=1)

    chosen = expert_ids.T[None, :, :] == jnp.arange(experts, dtype=jnp.int32)[:, None, None]
    dense = jnp.sum(jnp.where(chosen, gate_probs.T[None, :, :], 0.0), axis=1)
    x0, x1 = spread(shuffle(tokens))
    pair = jnp.concatenate([w_gate[0], w_up[0]], axis=1)
    wgu = gather_rows(pair)
    wgu = lax.optimization_barrier(jnp.concatenate(wgu, axis=0))
    wd = gather_rows(w_down[0])
    wd = lax.optimization_barrier(jnp.concatenate(in_order(wd, own), axis=0))
    c0, c1 = spread(cotangent)
    near = [dense]
    for m in range(1, pairs):
        near.append(send(dense, "expert", 2 * m))
    near = lax.optimization_barrier(jnp.stack(near))
    far = send(near, "expert", 1)
    p0 = lax.dynamic_index_in_dim(near, me, 1, False).reshape(pairs * rows, 1)
    p1 = lax.dynamic_index_in_dim(far, me, 1, False).reshape(pairs * rows, 1)

    def project(x):
        return lax.optimization_barrier(mm(x, wgu, ((1,), (0,))))

    def forward(pre, p):
        hidden = (jax.nn.silu(pre[:, :hid]) * pre[:, hid:]).astype(BF)
        result = mm(hidden, wd, ((1,), (0,))).astype(BF)
        part = (p * result.astype(F32)).astype(BF)
        return hidden, result, part

    def backward(c, p, pre):
        out_grad = (p * c.astype(F32)).astype(BF)
        hidden_grad = mm(out_grad, wd, ((1,), (1,)))
        gate, up = pre[:, :hid], pre[:, hid:]
        sig = jax.nn.sigmoid(gate)
        gate_grad = (hidden_grad * up * sig * (1.0 + gate * (1.0 - sig))).astype(BF)
        up_grad = (hidden_grad * (gate * sig)).astype(BF)
        pre_grad = jnp.concatenate([gate_grad, up_grad], axis=1)
        return lax.optimization_barrier((out_grad, pre_grad))

    def rowgrad(pre_grad):
        return lax.optimization_barrier(mm(pre_grad, wgu, ((1,), (1,))).astype(BF))

    q0, q1 = project(x0), project(x1)
    h1, r1, m1 = forward(q1, p1)
    h0, r0, m0 = forward(q0, p0)
    mixed = collect(m0, m1, rows)
    q0, h0, r0, q1, h1, r1 = lax.optimization_barrier((q0, h0, r0, q1, h1, r1))
    p0, p1 = lax.optimization_barrier((p0, p1))
    o0, g0 = backward(c0, p0, q0)
    o1, g1 = backward(c1, p1, q1)
    b1, b0 = rowgrad(g1), rowgrad(g0)
    t0, r0, t1, r1, _ = lax.optimization_barrier((c0, r0, c1, r1, b0))
    i0 = jnp.sum(t0.astype(F32) * r0.astype(F32), axis=1)
    i1 = jnp.sum(t1.astype(F32) * r1.astype(F32), axis=1)
    input_grad = shuffle(collect(b0, b1, rows))
    down_part = mm(h0, o0, ((0,), (0,))) + mm(h1, o1, ((0,), (0,)))
    down_part = (down_part * scale).astype(BF)
    down_parts = [down_part[j * dhid : (j + 1) * dhid] for j in range(data_devices)]
    down_parts = in_order(down_parts, own)
    down_grad = scatter_rows(down_parts)
    gu_part = mm(x0, g0, ((0,), (0,))) + mm(x1, g1, ((0,), (0,)))
    gu_part = (gu_part * scale).astype(BF)
    gu_grad = scatter_rows([gu_part[j * dwidth : (j + 1) * dwidth] for j in range(data_devices)])

    mine = i0.reshape(pairs, rows)
    other = send(i1.reshape(pairs, rows), "expert", 1)
    both = jnp.stack([mine, other], axis=1)
    prob_grad = jnp.zeros(expert_ids.shape, F32)
    for m in range(pairs):
        got = both[m] if m == 0 else send(both[m], "expert", 2 * m)
        for j in range(2):
            hit = expert_ids == (me ^ (2 * m + j))
            prob_grad = prob_grad + jnp.where(hit, got[j][:, None], 0.0)
    return (
        mixed,
        input_grad,
        prob_grad,
        gu_grad[None, :, :hid],
        gu_grad[None, :, hid:],
        down_grad[None],
    )


def solution(mesh):
    both = P(("dp", "expert"), None)
    weight = P("expert", "dp", None)
    return jax.shard_map(
        per_device,
        mesh=mesh,
        in_specs=(both, both, both, weight, weight, weight, both),
        out_specs=(both, both, both, weight, weight, weight),
        check_vma=False,
    )
```

time: 221 us -> 165 us (0.75)
  waiting for transfers between devices: 126 us -> 79.3 us
  starting transfers between devices: 18.7 us -> 59.3 us
  local copies, waits for them, and re-layouts: 24.5 us -> 1.31 us
  matrix products: 30.6 us -> 13 us
  between operations: 14.4 us -> 1.15 us
  other arithmetic: 6.42 us -> 10.8 us
    all_to_all x4 -> x0, waiting for transfers between devices: 106 us -> none  [the longest x1 29.5 us: per_device(): lax.all_to_all(result, 'expert', split_axis=0, concat_axis=0, tiled=True)]
    ppermute x0 -> x40, waiting for transfers between devices: none -> 79.3 us  [send(): return lax.ppermute(x, axis, pairs)]
    ppermute x0 -> x40, starting transfers between devices: none -> 59.3 us  [send(): return lax.ppermute(x, axis, pairs)]
    all_to_all x4 -> x0, starting transfers between devices: 18.3 us -> none  [the longest x1 6.49 us: per_device(): lax.all_to_all(send_rows, 'expert', split_axis=0, concat_axis=0, tiled=True)]
    all_gather x3 -> x0, waiting for transfers between devices: 17.7 us -> none  [the longest x1 12.9 us: per_device(): lax.all_gather(w_down, 'dp', axis=1, tiled=True)]
    dot_general x10 -> x12, matrix products: 30.6 us -> 13 us  [mm(): lax.dot_general(a, b, ((dims[0], dims[1]), ((), ())), preferred_element_t...]
    gather x4 -> x0, local copies, waits for them, and re-layouts: 12 us -> none  [the longest x1 3.6 us: per_device(): send_grads = out_pairs[slot_owner].reshape(experts, capacity, model_width)]
    mul x5 -> x0, local copies, waits for them, and re-layouts: 4.19 us -> none  [the longest x2 3.86 us: per_device(): gate_probs[:, :, None] * cotangent.astype(jnp.float32)[:, None, :]]
  transfers between devices with their start and end apart: 10 -> 40, of which waited for: 6 -> 16; matrix products, arithmetic and copies ran while one was open for 20% -> 13% of each run, Pallas kernels for 0% -> 0%
where the time goes in v1:
time: 165 us
  waiting for transfers between devices  79.3 us (48%)
  starting transfers between devices  59.3 us (36%)
  matrix products  13 us (8%)
  other arithmetic  10.8 us (7%)
    ppermute x40, waiting for transfers between devices, send(): return lax.ppermute(x, axis, pairs)  79.3 us
    ppermute x40, starting transfers between devices, send(): return lax.ppermute(x, axis, pairs)  59.3 us
    dot_general x12, matrix products, mm(): lax.dot_general(a, b, ((dims[0], dims[1]), ((), ())), preferred_element_t...  13 us
  transfers between devices with their start and end apart: 40, of which 16 were waited for; matrix products, arithmetic and copies ran while one was open for 13% of the time, Pallas kernels for 0%

profile of v1, /device:TPU:0, one launch (start us, length us, event | category | flops | bytes accessed | tf_op | source)
XLA Modules:
  0.0 164.8 jit_solution(4673135353185011415)
XLA Ops:
  0.7 0.8 select_reduce_fusion
  1.4 5.1 %collective-permute-start.2 = (f32[8,128]{1,0:T(8,128)S(1)}, f32[8,128]{1,0:T(8,128)S(1)}, u32[]{:S(2)}, u32[]{:S(2)}) collective-permute-start(f32[8,128]{1,0:T(8,128)S(1)} %select_reduce_fusion), channel_id=1, source_target_pairs={{0,6},{1,7},{2,4},{3,5},{4,2},{5,3},{6,0},{7,1},{8,14},{9,15},{10,... | collective-permute-start | bytes 12296 | tf_op jit(solution)/shard_map/ppermute | solution.py:13
  6.5 0.6 collective-permute-start
  7.1 1.0 broadcast_select_fusion.32
  8.1 0.7 collective-permute-start.5
  8.8 4.2 %collective-permute-start.4 = (bf16[128,1024]{1,0:T(8,128)(2,1)S(1)}, bf16[128,1024]{1,0:T(8,128)(2,1)S(1)}, u32[]{:S(2)}, u32[]{:S(2)}) collective-permute-start(bf16[128,1024]{1,0:T(8,128)(2,1)S(1)} %pad_maximum_fusion.6), channel_id=1, source_target_pairs={{0,4},{1,5},{2,6},{3,7},{4,0},{5,1},{6,2},{7,3},{8,12},{9,13},{10,... | collective-permute-start | bytes 786440 | tf_op jit(solution)/shard_map/ppermute | solution.py:13
  13.0 2.0 %pad_maximum_fusion.5 = (bf16[256,1024]{1,0:T(8,128)(2,1)S(1)}, bf16[1024,1024]{1,0:T(8,128)(2,1)}) fusion(bf16[256,512]{1,0:T(8,128)(2,1)} %bitcast.74, bf16[256,512]{1,0:T(8,128)(2,1)} %bitcast.75), kind=kLoop, calls=%fused_computation.30 | loop fusion | flops 1048575 | bytes 1572864 | tf_op jit(solution)/shard_map/concatenate | solution.py:109
  14.9 1.5 collective-permute-start.11
  16.4 1.5 collective-permute-start.13
  18.0 3.9 %collective-permute-done.11 = bf16[128,1024]{1,0:T(8,128)(2,1)S(1)} collective-permute-done((bf16[128,1024]{1,0:T(8,128)(2,1)S(1)}, bf16[128,1024]{1,0:T(8,128)(2,1)S(1)}, u32[]{:S(2)}, u32[]{:S(2)}) %collective-permute-start.11) | collective-permute-done | bytes 262176 | tf_op jit(solution)/shard_map/ppermute | solution.py:13
  22.2 1.6 collective-permute-start.12
  23.8 1.6 collective-permute-start.14
  25.3 2.1 %collective-permute-done.12 = bf16[64,1024]{1,0:T(8,128)(2,1)S(1)} collective-permute-done((bf16[64,1024]{1,0:T(8,128)(2,1)S(1)}, bf16[64,1024]{1,0:T(8,128)(2,1)S(1)}, u32[]{:S(2)}, u32[]{:S(2)}) %collective-permute-start.12) | collective-permute-done | bytes 131104 | tf_op jit(solution)/shard_map/ppermute | solution.py:13
  27.5 1.5 collective-permute-start.7
  29.0 0.7 collective-permute-done.4
  29.7 2.4 %collective-permute-start.22 = (bf16[128,1024]{1,0:T(8,128)(2,1)S(1)}, bf16[128,1024]{1,0:T(8,128)(2,1)S(1)}, u32[]{:S(2)}, u32[]{:S(2)}) collective-permute-start(bf16[128,1024]{1,0:T(8,128)(2,1)S(1)} %copy-done.1), channel_id=1, source_target_pairs={{0,4},{1,5},{2,6},{3,7},{4,0},{5,1},{6,2},{7,3},{8,12},{9,13},{10,... | collective-permute-start | bytes 786440 | tf_op jit(solution)/shard_map/ppermute | solution.py:13
  32.1 1.3 collective-permute-start.6
  33.5 1.6 collective-permute-start.8
  35.2 7.7 %collective-permute-done.22 = bf16[128,1024]{1,0:T(8,128)(2,1)S(1)} collective-permute-done((bf16[128,1024]{1,0:T(8,128)(2,1)S(1)}, bf16[128,1024]{1,0:T(8,128)(2,1)S(1)}, u32[]{:S(2)}, u32[]{:S(2)}) %collective-permute-start.22) | collective-permute-done | bytes 262176 | tf_op jit(solution)/shard_map/ppermute | solution.py:13
  42.9 0.7 collective-permute-start.23
  43.5 1.6 collective-permute-done.6
  45.1 1.3 collective-permute-start.24
  46.5 2.7 %collective-permute-start.21 = (bf16[128,1024]{1,0:T(8,128)(2,1)S(1)}, bf16[128,1024]{1,0:T(8,128)(2,1)S(1)}, u32[]{:S(2)}, u32[]{:S(2)}) collective-permute-start(bf16[128,1024]{1,0:T(8,128)(2,1)S(1)} %copy-done.1), channel_id=1, source_target_pairs={{0,2},{1,3},{2,0},{3,1},{4,6},{5,7},{6,4},{7,5},{8,10},{9,11},{10,... | collective-permute-start | bytes 786440 | tf_op jit(solution)/shard_map/ppermute | solution.py:13
  49.4 1.3 collective-permute-start.9
  50.7 1.6 collective-permute-start.10
  52.3 3.9 %collective-permute-done.24 = bf16[128,1024]{1,0:T(8,128)(2,1)S(1)} collective-permute-done((bf16[128,1024]{1,0:T(8,128)(2,1)S(1)}, bf16[128,1024]{1,0:T(8,128)(2,1)S(1)}, u32[]{:S(2)}, u32[]{:S(2)}) %collective-permute-start.24) | collective-permute-done | bytes 262176 | tf_op jit(solution)/shard_map/ppermute | solution.py:13
  56.2 3.0 %collective-permute-done.21 = bf16[128,1024]{1,0:T(8,128)(2,1)S(1)} collective-permute-done((bf16[128,1024]{1,0:T(8,128)(2,1)S(1)}, bf16[128,1024]{1,0:T(8,128)(2,1)S(1)}, u32[]{:S(2)}, u32[]{:S(2)}) %collective-permute-start.21) | collective-permute-done | bytes 262176 | tf_op jit(solution)/shard_map/ppermute | solution.py:13
  59.7 1.3 fusion.7
  61.3 0.7 convolution_convert_fusion.3
  62.1 1.3 fusion.8
  63.7 0.7 multiply_convert_fusion.4
  64.7 1.0 multiply_convert_fusion.7
  65.9 1.3 convolution_convert_fusion
  67.2 0.6 collective-permute-start.26
  67.7 1.0 multiply_convert_fusion.9
  68.9 1.3 convolution_convert_fusion.1
  71.0 1.3 fusion.9
  72.3 1.6 multiply_convert_fusion
  74.0 2.5 %collective-permute-start.36 = (bf16[256,1024]{1,0:T(8,128)(2,1)S(1)}, bf16[256,1024]{1,0:T(8,128)(2,1)S(1)}, u32[]{:S(2)}, u32[]{:S(2)}) collective-permute-start(bf16[256,1024]{1,0:T(8,128)(2,1)S(1)} %get-tuple-element.43), channel_id=1, source_target_pairs={{0,24},{8,16},{16,8},{24,0},{1,25},{9,17},{17,9},{25,1},{2,26},{10... | collective-permute-start | bytes 1572872 | tf_op jit(solution)/shard_map/ppermute | solution.py:13
  76.5 0.7 fusion.10
  77.3 0.7 multiply_convert_fusion.1
  78.1 0.5 collective-permute-start.39
  78.6 1.5 collective-permute-start.38
  80.2 2.7 %collective-permute-start.33 = (f32[2,128]{1,0:T(2,128)S(1)}, f32[2,128]{1,0:T(2,128)S(1)}, u32[]{:S(2)}, u32[]{:S(2)}) collective-permute-start(f32[2,128]{1,0:T(2,128)S(1)} %get-tuple-element.72), channel_id=1, source_target_pairs={{0,6},{1,7},{2,4},{3,5},{4,2},{5,3},{6,0},{7,1},{8,14},{9,15},{10,... | collective-permute-start | bytes 3080 | tf_op jit(solution)/shard_map/ppermute | solution.py:13
  82.9 2.7 %collective-permute-done.33 = f32[2,128]{1,0:T(2,128)S(1)} collective-permute-done((f32[2,128]{1,0:T(2,128)S(1)}, f32[2,128]{1,0:T(2,128)S(1)}, u32[]{:S(2)}, u32[]{:S(2)}) %collective-permute-start.33) | collective-permute-done | bytes 1056 | tf_op jit(solution)/shard_map/ppermute | solution.py:13
  85.6 4.5 %collective-permute-done.32 = f32[2,128]{1,0:T(2,128)S(1)} collective-permute-done((f32[2,128]{1,0:T(2,128)S(1)}, f32[2,128]{1,0:T(2,128)S(1)}, u32[]{:S(2)}, u32[]{:S(2)}) %collective-permute-start.32) | collective-permute-done | bytes 1056 | tf_op jit(solution)/shard_map/ppermute | solution.py:13
  90.4 3.3 %collective-permute-done.31 = f32[2,128]{1,0:T(2,128)S(1)} collective-permute-done((f32[2,128]{1,0:T(2,128)S(1)}, f32[2,128]{1,0:T(2,128)S(1)}, u32[]{:S(2)}, u32[]{:S(2)}) %collective-permute-start.31) | collective-permute-done | bytes 1056 | tf_op jit(solution)/shard_map/ppermute | solution.py:13
  94.2 0.9 collective-permute-done.39
  95.0 1.5 collective-permute-start.34
  96.5 4.1 %collective-permute-done.38 = bf16[128,1024]{1,0:T(8,128)(2,1)S(1)} collective-permute-done((bf16[128,1024]{1,0:T(8,128)(2,1)S(1)}, bf16[128,1024]{1,0:T(8,128)(2,1)S(1)}, u32[]{:S(2)}, u32[]{:S(2)}) %collective-permute-start.38) | collective-permute-done | bytes 262176 | tf_op jit(solution)/shard_map/ppermute | solution.py:13
  100.6 1.5 collective-permute-start.37
  102.1 0.6 select_add_fusion
  102.7 11.3 %collective-permute-done.37 = bf16[128,1024]{1,0:T(8,128)(2,1)S(1)} collective-permute-done((bf16[128,1024]{1,0:T(8,128)(2,1)S(1)}, bf16[128,1024]{1,0:T(8,128)(2,1)S(1)}, u32[]{:S(2)}, u32[]{:S(2)}) %collective-permute-start.37) | collective-permute-done | bytes 262176 | tf_op jit(solution)/shard_map/ppermute | solution.py:13
  114.0 1.0 fusion.2
  115.4 0.8 slice_bitcast_fusion
  116.7 2.7 %collective-permute-start.29 = (bf16[128,1024]{1,0:T(8,128)(2,1)S(1)}, bf16[128,1024]{1,0:T(8,128)(2,1)S(1)}, u32[]{:S(2)}, u32[]{:S(2)}) collective-permute-start(bf16[128,1024]{1,0:T(8,128)(2,1)S(1)} %get-tuple-element.49), channel_id=1, source_target_pairs={{0,6},{1,7},{2,4},{3,5},{4,2},{5,3},{6,0},{7,1},{8,14},{9,15},{10,... | collective-permute-start | bytes 786440 | tf_op jit(solution)/shard_map/ppermute | solution.py:13
  119.5 1.7 %collective-permute-start.27 = (bf16[128,1024]{1,0:T(8,128)(2,1)S(1)}, bf16[128,1024]{1,0:T(8,128)(2,1)S(1)}, u32[]{:S(2)}, u32[]{:S(2)}) collective-permute-start(bf16[128,1024]{1,0:T(8,128)(2,1)S(1)} %get-tuple-element.48), channel_id=1, source_target_pairs={{0,2},{1,3},{2,0},{3,1},{4,6},{5,7},{6,4},{7,5},{8,10},{9,11},{10,... | collective-permute-start | bytes 786440 | tf_op jit(solution)/shard_map/ppermute | solution.py:13
  121.6 2.7 %collective-permute-start.20 = (bf16[128,1024]{1,0:T(8,128)(2,1)S(1)}, bf16[128,1024]{1,0:T(8,128)(2,1)S(1)}, u32[]{:S(2)}, u32[]{:S(2)}) collective-permute-start(bf16[128,1024]{1,0:T(8,128)(2,1)S(1)} %get-tuple-element.52), channel_id=1, source_target_pairs={{0,6},{1,7},{2,4},{3,5},{4,2},{5,3},{6,0},{7,1},{8,14},{9,15},{10,... | collective-permute-start | bytes 786440 | tf_op jit(solution)/shard_map/ppermute | solution.py:13
  124.4 3.6 %collective-permute-done.29 = bf16[128,1024]{1,0:T(8,128)(2,1)S(1)} collective-permute-done((bf16[128,1024]{1,0:T(8,128)(2,1)S(1)}, bf16[128,1024]{1,0:T(8,128)(2,1)S(1)}, u32[]{:S(2)}, u32[]{:S(2)}) %collective-permute-start.29) | collective-permute-done | bytes 262176 | tf_op jit(solution)/shard_map/ppermute | solution.py:13
  127.9 8.8 %collective-permute-start.18 = (bf16[128,1024]{1,0:T(8,128)(2,1)S(1)}, bf16[128,1024]{1,0:T(8,128)(2,1)S(1)}, u32[]{:S(2)}, u32[]{:S(2)}) collective-permute-start(bf16[128,1024]{1,0:T(8,128)(2,1)S(1)} %get-tuple-element.51), channel_id=1, source_target_pairs={{0,2},{1,3},{2,0},{3,1},{4,6},{5,7},{6,4},{7,5},{8,10},{9,11},{10,... | collective-permute-start | bytes 786440 | tf_op jit(solution)/shard_map/ppermute | solution.py:13
  136.8 16.3 %collective-permute-done.28 = bf16[128,1024]{1,0:T(8,128)(2,1)S(1)} collective-permute-done((bf16[128,1024]{1,0:T(8,128)(2,1)S(1)}, bf16[128,1024]{1,0:T(8,128)(2,1)S(1)}, u32[]{:S(2)}, u32[]{:S(2)}) %collective-permute-start.28) | collective-permute-done | bytes 262176 | tf_op jit(solution)/shard_map/ppermute | solution.py:13
  153.3 0.7 pad_maximum_fusion.7
  154.0 9.9 %collective-permute-done.19 = bf16[128,1024]{1,0:T(8,128)(2,1)S(1)} collective-permute-done((bf16[128,1024]{1,0:T(8,128)(2,1)S(1)}, bf16[128,1024]{1,0:T(8,128)(2,1)S(1)}, u32[]{:S(2)}, u32[]{:S(2)}) %collective-permute-start.19) | collective-permute-done | bytes 262176 | tf_op jit(solution)/shard_map/ppermute | solution.py:13
  163.9 0.9 add_convert_fusion.5
  (89 shorter events, 5.8 us)
Async XLA Ops:
  0.6 14.3 %copy-start = (bf16[1,128,1024]{2,1,0:T(8,128)(2,1)S(1)}, bf16[1,128,1024]{2,1,0:T(8,128)(2,1)}, u32[]{:S(2)}) copy-start(bf16[1,128,1024]{2,1,0:T(8,128)(2,1)} %param.12) | copy-start | bytes 786436
  0.6 29.0 %copy-start.1 = (bf16[128,1024]{1,0:T(8,128)(2,1)S(1)}, bf16[128,1024]{1,0:T(8,128)(2,1)}, u32[]{:S(2)}) copy-start(bf16[128,1024]{1,0:T(8,128)(2,1)} %param.13) | copy-start | bytes 786436
  1.4 13.5 %collective-permute-start.2 = (f32[8,128]{1,0:T(8,128)S(1)}, f32[8,128]{1,0:T(8,128)S(1)}, u32[]{:S(2)}, u32[]{:S(2)}) collective-permute-start(f32[8,128]{1,0:T(8,128)S(1)} %select_reduce_fusion), channel_id=1, source_target_pairs={{0,6},{1,7},{2,4},{3,5},{4,2},{5,3},{6,0},{7,1},{8,14},{9,15},{10,... | collective-permute-start | bytes 12296 | tf_op jit(solution)/shard_map/ppermute | solution.py:13
  6.5 9.9 %collective-permute-start.1 = (f32[8,128]{1,0:T(8,128)S(1)}, f32[8,128]{1,0:T(8,128)S(1)}, u32[]{:S(2)}, u32[]{:S(2)}) collective-permute-start(f32[8,128]{1,0:T(8,128)S(1)} %select_reduce_fusion), channel_id=1, source_target_pairs={{0,4},{1,5},{2,6},{3,7},{4,0},{5,1},{6,2},{7,3},{8,12},{9,13},{10,... | collective-permute-start | bytes 12296 | tf_op jit(solution)/shard_map/ppermute | solution.py:13
  6.5 11.4 %collective-permute-start = (f32[8,128]{1,0:T(8,128)S(1)}, f32[8,128]{1,0:T(8,128)S(1)}, u32[]{:S(2)}, u32[]{:S(2)}) collective-permute-start(f32[8,128]{1,0:T(8,128)S(1)} %select_reduce_fusion), channel_id=1, source_target_pairs={{0,2},{1,3},{2,0},{3,1},{4,6},{5,7},{6,4},{7,5},{8,10},{9,11},{10,... | collective-permute-start | bytes 12296 | tf_op jit(solution)/shard_map/ppermute | solution.py:13
  8.1 25.4 %collective-permute-start.5 = (bf16[128,1024]{1,0:T(8,128)(2,1)S(1)}, bf16[128,1024]{1,0:T(8,128)(2,1)S(1)}, u32[]{:S(2)}, u32[]{:S(2)}) collective-permute-start(bf16[128,1024]{1,0:T(8,128)(2,1)S(1)} %pad_maximum_fusion.6), channel_id=1, source_target_pairs={{2,4},{3,5},{4,2},{5,3},{10,12},{11,13},{12,10},{13,11},{18,20},{1... | collective-permute-start | bytes 786440 | tf_op jit(solution)/shard_map/ppermute | solution.py:13
  8.8 20.9 %collective-permute-start.4 = (bf16[128,1024]{1,0:T(8,128)(2,1)S(1)}, bf16[128,1024]{1,0:T(8,128)(2,1)S(1)}, u32[]{:S(2)}, u32[]{:S(2)}) collective-permute-start(bf16[128,1024]{1,0:T(8,128)(2,1)S(1)} %pad_maximum_fusion.6), channel_id=1, source_target_pairs={{0,4},{1,5},{2,6},{3,7},{4,0},{5,1},{6,2},{7,3},{8,12},{9,13},{10,... | collective-permute-start | bytes 786440 | tf_op jit(solution)/shard_map/ppermute | solution.py:13
  14.9 6.9 %collective-permute-start.11 = (bf16[128,1024]{1,0:T(8,128)(2,1)S(1)}, bf16[128,1024]{1,0:T(8,128)(2,1)S(1)}, u32[]{:S(2)}, u32[]{:S(2)}) collective-permute-start(bf16[128,1024]{1,0:T(8,128)(2,1)S(1)} %bitcast.76), channel_id=1, source_target_pairs={{0,16},{8,24},{16,0},{24,8},{1,17},{9,25},{17,1},{25,9},{2,18},{10... | collective-permute-start | bytes 786440 | tf_op jit(solution)/shard_map/ppermute | solution.py:13
  16.4 7.3 %collective-permute-start.13 = (bf16[128,1024]{1,0:T(8,128)(2,1)S(1)}, bf16[128,1024]{1,0:T(8,128)(2,1)S(1)}, u32[]{:S(2)}, u32[]{:S(2)}) collective-permute-start(bf16[128,1024]{1,0:T(8,128)(2,1)S(1)} %bitcast.77), channel_id=1, source_target_pairs={{0,8},{8,0},{16,24},{24,16},{1,9},{9,1},{17,25},{25,17},{2,10},{10... | collective-permute-start | bytes 786440 | tf_op jit(solution)/shard_map/ppermute | solution.py:13
  17.9 4.2 %collective-permute-start.15 = (f32[4,8,128]{2,1,0:T(8,128)S(1)}, f32[4,8,128]{2,1,0:T(8,128)S(1)}, u32[]{:S(2)}, u32[]{:S(2)}) collective-permute-start(f32[4,8,128]{2,1,0:T(8,128)S(1)} %pad_maximum_fusion.8), channel_id=1, source_target_pairs={{0,1},{1,0},{2,3},{3,2},{4,5},{5,4},{6,7},{7,6},{8,9},{9,8},{10,11... | collective-permute-start | bytes 49160 | tf_op jit(solution)/shard_map/ppermute | solution.py:13
  21.8 24.6 %collective-permute-start.3 = (bf16[128,1024]{1,0:T(8,128)(2,1)S(1)}, bf16[128,1024]{1,0:T(8,128)(2,1)S(1)}, u32[]{:S(2)}, u32[]{:S(2)}) collective-permute-start(bf16[128,1024]{1,0:T(8,128)(2,1)S(1)} %pad_maximum_fusion.6), channel_id=1, source_target_pairs={{0,2},{1,3},{2,0},{3,1},{4,6},{5,7},{6,4},{7,5},{8,10},{9,11},{10,... | collective-permute-start | bytes 786440 | tf_op jit(solution)/shard_map/ppermute | solution.py:13
  22.2 5.3 %collective-permute-start.12 = (bf16[64,1024]{1,0:T(8,128)(2,1)S(1)}, bf16[64,1024]{1,0:T(8,128)(2,1)S(1)}, u32[]{:S(2)}, u32[]{:S(2)}) collective-permute-start(bf16[64,1024]{1,0:T(8,128)(2,1)S(1)} %slice.209), channel_id=1, source_target_pairs={{0,8},{8,0},{16,24},{24,16},{1,9},{9,1},{17,25},{25,17},{2,10},{10... | collective-permute-start | bytes 393224 | tf_op jit(solution)/shard_map/ppermute | solution.py:13
  23.8 8.3 %collective-permute-start.14 = (bf16[64,1024]{1,0:T(8,128)(2,1)S(1)}, bf16[64,1024]{1,0:T(8,128)(2,1)S(1)}, u32[]{:S(2)}, u32[]{:S(2)}) collective-permute-start(bf16[64,1024]{1,0:T(8,128)(2,1)S(1)} %slice.210), channel_id=1, source_target_pairs={{0,16},{8,24},{16,0},{24,8},{1,17},{9,25},{17,1},{25,9},{2,18},{10... | collective-permute-start | bytes 393224 | tf_op jit(solution)/shard_map/ppermute | solution.py:13
  27.5 21.9 %collective-permute-start.7 = (bf16[256,1024]{1,0:T(8,128)(2,1)S(1)}, bf16[256,1024]{1,0:T(8,128)(2,1)S(1)}, u32[]{:S(2)}, u32[]{:S(2)}) collective-permute-start(bf16[256,1024]{1,0:T(8,128)(2,1)S(1)} %get-tuple-element.60), channel_id=1, source_target_pairs={{0,8},{8,0},{16,24},{24,16},{1,9},{9,1},{17,25},{25,17},{2,10},{10... | collective-permute-start | bytes 1572872 | tf_op jit(solution)/shard_map/ppermute | solution.py:13
  29.7 13.2 %collective-permute-start.22 = (bf16[128,1024]{1,0:T(8,128)(2,1)S(1)}, bf16[128,1024]{1,0:T(8,128)(2,1)S(1)}, u32[]{:S(2)}, u32[]{:S(2)}) collective-permute-start(bf16[128,1024]{1,0:T(8,128)(2,1)S(1)} %copy-done.1), channel_id=1, source_target_pairs={{0,4},{1,5},{2,6},{3,7},{4,0},{5,1},{6,2},{7,3},{8,12},{9,13},{10,... | collective-permute-start | bytes 786440 | tf_op jit(solution)/shard_map/ppermute | solution.py:13
  32.1 13.0 %collective-permute-start.6 = (bf16[128,1024]{1,0:T(8,128)(2,1)S(1)}, bf16[128,1024]{1,0:T(8,128)(2,1)S(1)}, u32[]{:S(2)}, u32[]{:S(2)}) collective-permute-start(bf16[128,1024]{1,0:T(8,128)(2,1)S(1)} %collective-permute-done.4), channel_id=1, source_target_pairs={{2,0},{3,1},{4,6},{5,7},{10,8},{11,9},{12,14},{13,15},{18,16},{19,... | collective-permute-start | bytes 786440 | tf_op jit(solution)/shard_map/ppermute | solution.py:13
  33.5 15.7 %collective-permute-start.8 = (bf16[256,1024]{1,0:T(8,128)(2,1)S(1)}, bf16[256,1024]{1,0:T(8,128)(2,1)S(1)}, u32[]{:S(2)}, u32[]{:S(2)}) collective-permute-start(bf16[256,1024]{1,0:T(8,128)(2,1)S(1)} %get-tuple-element.60), channel_id=1, source_target_pairs={{0,16},{8,24},{16,0},{24,8},{1,17},{9,25},{17,1},{25,9},{2,18},{10... | collective-permute-start | bytes 1572872 | tf_op jit(solution)/shard_map/ppermute | solution.py:13
  42.9 7.9 %collective-permute-start.23 = (bf16[128,1024]{1,0:T(8,128)(2,1)S(1)}, bf16[128,1024]{1,0:T(8,128)(2,1)S(1)}, u32[]{:S(2)}, u32[]{:S(2)}) collective-permute-start(bf16[128,1024]{1,0:T(8,128)(2,1)S(1)} %copy-done.1), channel_id=1, source_target_pairs={{2,4},{3,5},{4,2},{5,3},{10,12},{11,13},{12,10},{13,11},{18,20},{1... | collective-permute-start | bytes 786440 | tf_op jit(solution)/shard_map/ppermute | solution.py:13
  45.1 11.1 %collective-permute-start.24 = (bf16[128,1024]{1,0:T(8,128)(2,1)S(1)}, bf16[128,1024]{1,0:T(8,128)(2,1)S(1)}, u32[]{:S(2)}, u32[]{:S(2)}) collective-permute-start(bf16[128,1024]{1,0:T(8,128)(2,1)S(1)} %collective-permute-done.22), channel_id=1, source_target_pairs={{2,0},{3,1},{4,6},{5,7},{10,8},{11,9},{12,14},{13,15},{18,16},{19,... | collective-permute-start | bytes 786440 | tf_op jit(solution)/shard_map/ppermute | solution.py:13
  46.5 12.7 %collective-permute-start.21 = (bf16[128,1024]{1,0:T(8,128)(2,1)S(1)}, bf16[128,1024]{1,0:T(8,128)(2,1)S(1)}, u32[]{:S(2)}, u32[]{:S(2)}) collective-permute-start(bf16[128,1024]{1,0:T(8,128)(2,1)S(1)} %copy-done.1), channel_id=1, source_target_pairs={{0,2},{1,3},{2,0},{3,1},{4,6},{5,7},{6,4},{7,5},{8,10},{9,11},{10,... | collective-permute-start | bytes 786440 | tf_op jit(solution)/shard_map/ppermute | solution.py:13
  49.3 12.8 %collective-permute-start.16 = (bf16[512,1024]{1,0:T(8,128)(2,1)S(1)}, bf16[512,1024]{1,0:T(8,128)(2,1)S(1)}, u32[]{:S(2)}, u32[]{:S(2)}) collective-permute-start(bf16[512,1024]{1,0:T(8,128)(2,1)S(1)} %pad_maximum_fusion), channel_id=1, source_target_pairs={{0,1},{1,0},{2,3},{3,2},{4,5},{5,4},{6,7},{7,6},{8,9},{9,8},{10,11... | collective-permute-start | bytes 3145736 | tf_op jit(solution)/shard_map/ppermute | solution.py:13
  49.4 10.3 %collective-permute-start.9 = (bf16[128,1024]{1,0:T(8,128)(2,1)S(1)}, bf16[128,1024]{1,0:T(8,128)(2,1)S(1)}, u32[]{:S(2)}, u32[]{:S(2)}) collective-permute-start(bf16[128,1024]{1,0:T(8,128)(2,1)S(1)} %slice.205), channel_id=1, source_target_pairs={{0,8},{8,0},{16,24},{24,16},{1,9},{9,1},{17,25},{25,17},{2,10},{10... | collective-permute-start | bytes 786440 | tf_op jit(solution)/shard_map/ppermute | solution.py:13
  50.7 9.0 %collective-permute-start.10 = (bf16[128,1024]{1,0:T(8,128)(2,1)S(1)}, bf16[128,1024]{1,0:T(8,128)(2,1)S(1)}, u32[]{:S(2)}, u32[]{:S(2)}) collective-permute-start(bf16[128,1024]{1,0:T(8,128)(2,1)S(1)} %slice.206), channel_id=1, source_target_pairs={{0,16},{8,24},{16,0},{24,8},{1,17},{9,25},{17,1},{25,9},{2,18},{10... | collective-permute-start | bytes 786440 | tf_op jit(solution)/shard_map/ppermute | solution.py:13
  56.2 3.4 %copy-start.2 = (bf16[1024,1024]{1,0:T(8,128)(2,1)S(1)}, bf16[1024,1024]{1,0:T(8,128)(2,1)}, u32[]{:S(2)}) copy-start(bf16[1024,1024]{1,0:T(8,128)(2,1)} %get-tuple-element.61) | copy-start | bytes 6291460
  59.2 5.2 %collective-permute-start.25 = (bf16[512,1024]{1,0:T(8,128)(2,1)S(1)}, bf16[512,1024]{1,0:T(8,128)(2,1)S(1)}, u32[]{:S(2)}, u32[]{:S(2)}) collective-permute-start(bf16[512,1024]{1,0:T(8,128)(2,1)S(1)} %pad_maximum_fusion.2), channel_id=1, source_target_pairs={{0,1},{1,0},{2,3},{3,2},{4,5},{5,4},{6,7},{7,6},{8,9},{9,8},{10,11... | collective-permute-start | bytes 3145736 | tf_op jit(solution)/shard_map/ppermute | solution.py:13
  67.2 49.1 %collective-permute-start.26 = (bf16[512,1024]{1,0:T(8,128)(2,1)S(1)}, bf16[512,1024]{1,0:T(8,128)(2,1)S(1)}, u32[]{:S(2)}, u32[]{:S(2)}) collective-permute-start(bf16[512,1024]{1,0:T(8,128)(2,1)S(1)} %convolution_convert_fusion), channel_id=1, source_target_pairs={{0,1},{1,0},{2,3},{3,2},{4,5},{5,4},{6,7},{7,6},{8,9},{9,8},{10,11... | collective-permute-start | bytes 3145736 | tf_op jit(solution)/shard_map/ppermute | solution.py:13
  70.6 9.6 %collective-permute-start.30 = (f32[4,128]{1,0:T(4,128)S(1)}, f32[4,128]{1,0:T(4,128)S(1)}, u32[]{:S(2)}, u32[]{:S(2)}) collective-permute-start(f32[4,128]{1,0:T(4,128)S(1)} %bitcast.88), channel_id=1, source_target_pairs={{0,1},{1,0},{2,3},{3,2},{4,5},{5,4},{6,7},{7,6},{8,9},{9,8},{10,11... | collective-permute-start | bytes 6152 | tf_op jit(solution)/shard_map/ppermute | solution.py:13
  74.0 41.0 %collective-permute-start.36 = (bf16[256,1024]{1,0:T(8,128)(2,1)S(1)}, bf16[256,1024]{1,0:T(8,128)(2,1)S(1)}, u32[]{:S(2)}, u32[]{:S(2)}) collective-permute-start(bf16[256,1024]{1,0:T(8,128)(2,1)S(1)} %get-tuple-element.43), channel_id=1, source_target_pairs={{0,24},{8,16},{16,8},{24,0},{1,25},{9,17},{17,9},{25,1},{2,26},{10... | collective-permute-start | bytes 1572872 | tf_op jit(solution)/shard_map/ppermute | solution.py:13
  77.2 24.9 %copy-start.3 = (s32[128,4]{0,1:T(4,128)S(1)}, s32[128,4]{0,1:T(4,128)}, u32[]{:S(2)}) copy-start(s32[128,4]{0,1:T(4,128)} %param.8) | copy-start | bytes 6148
  78.1 16.9 %collective-permute-start.39 = (bf16[128,1024]{1,0:T(8,128)(2,1)S(1)}, bf16[128,1024]{1,0:T(8,128)(2,1)S(1)}, u32[]{:S(2)}, u32[]{:S(2)}) collective-permute-start(bf16[128,1024]{1,0:T(8,128)(2,1)S(1)} %get-tuple-element.47), channel_id=1, source_target_pairs={{0,24},{8,16},{16,8},{24,0},{1,25},{9,17},{17,9},{25,1},{2,26},{10... | collective-permute-start | bytes 786440 | tf_op jit(solution)/shard_map/ppermute | solution.py:13
  78.6 22.0 %collective-permute-start.38 = (bf16[128,1024]{1,0:T(8,128)(2,1)S(1)}, bf16[128,1024]{1,0:T(8,128)(2,1)S(1)}, u32[]{:S(2)}, u32[]{:S(2)}) collective-permute-start(bf16[128,1024]{1,0:T(8,128)(2,1)S(1)} %get-tuple-element.46), channel_id=1, source_target_pairs={{0,16},{8,24},{16,0},{24,8},{1,17},{9,25},{17,1},{25,9},{2,18},{10... | collective-permute-start | bytes 786440 | tf_op jit(solution)/shard_map/ppermute | solution.py:13
  80.2 5.4 %collective-permute-start.33 = (f32[2,128]{1,0:T(2,128)S(1)}, f32[2,128]{1,0:T(2,128)S(1)}, u32[]{:S(2)}, u32[]{:S(2)}) collective-permute-start(f32[2,128]{1,0:T(2,128)S(1)} %get-tuple-element.72), channel_id=1, source_target_pairs={{0,6},{1,7},{2,4},{3,5},{4,2},{5,3},{6,0},{7,1},{8,14},{9,15},{10,... | collective-permute-start | bytes 3080 | tf_op jit(solution)/shard_map/ppermute | solution.py:13
  85.6 4.5 %collective-permute-start.32 = (f32[2,128]{1,0:T(2,128)S(1)}, f32[2,128]{1,0:T(2,128)S(1)}, u32[]{:S(2)}, u32[]{:S(2)}) collective-permute-start(f32[2,128]{1,0:T(2,128)S(1)} %get-tuple-element.71), channel_id=1, source_target_pairs={{0,4},{1,5},{2,6},{3,7},{4,0},{5,1},{6,2},{7,3},{8,12},{9,13},{10,... | collective-permute-start | bytes 3080 | tf_op jit(solution)/shard_map/ppermute | solution.py:13
  90.1 3.6 %collective-permute-start.31 = (f32[2,128]{1,0:T(2,128)S(1)}, f32[2,128]{1,0:T(2,128)S(1)}, u32[]{:S(2)}, u32[]{:S(2)}) collective-permute-start(f32[2,128]{1,0:T(2,128)S(1)} %get-tuple-element.70), channel_id=1, source_target_pairs={{0,2},{1,3},{2,0},{3,1},{4,6},{5,7},{6,4},{7,5},{8,10},{9,11},{10,... | collective-permute-start | bytes 3080 | tf_op jit(solution)/shard_map/ppermute | solution.py:13
  93.6 21.4 %collective-permute-start.35 = (bf16[256,1024]{1,0:T(8,128)(2,1)S(1)}, bf16[256,1024]{1,0:T(8,128)(2,1)S(1)}, u32[]{:S(2)}, u32[]{:S(2)}) collective-permute-start(bf16[256,1024]{1,0:T(8,128)(2,1)S(1)} %get-tuple-element.44), channel_id=1, source_target_pairs={{0,16},{8,24},{16,0},{24,8},{1,17},{9,25},{17,1},{25,9},{2,18},{10... | collective-permute-start | bytes 1572872 | tf_op jit(solution)/shard_map/ppermute | solution.py:13
  95.0 20.0 %collective-permute-start.34 = (bf16[256,1024]{1,0:T(8,128)(2,1)S(1)}, bf16[256,1024]{1,0:T(8,128)(2,1)S(1)}, u32[]{:S(2)}, u32[]{:S(2)}) collective-permute-start(bf16[256,1024]{1,0:T(8,128)(2,1)S(1)} %get-tuple-element.42), channel_id=1, source_target_pairs={{0,8},{8,0},{16,24},{24,16},{1,9},{9,1},{17,25},{25,17},{2,10},{10... | collective-permute-start | bytes 1572872 | tf_op jit(solution)/shard_map/ppermute | solution.py:13
  100.6 13.4 %collective-permute-start.37 = (bf16[128,1024]{1,0:T(8,128)(2,1)S(1)}, bf16[128,1024]{1,0:T(8,128)(2,1)S(1)}, u32[]{:S(2)}, u32[]{:S(2)}) collective-permute-start(bf16[128,1024]{1,0:T(8,128)(2,1)S(1)} %get-tuple-element.45), channel_id=1, source_target_pairs={{0,8},{8,0},{16,24},{24,16},{1,9},{9,1},{17,25},{25,17},{2,10},{10... | collective-permute-start | bytes 786440 | tf_op jit(solution)/shard_map/ppermute | solution.py:13
  114.0 7.2 %collective-permute-start.17 = (bf16[512,1024]{1,0:T(8,128)(2,1)S(1)}, bf16[512,1024]{1,0:T(8,128)(2,1)S(1)}, u32[]{:S(2)}, u32[]{:S(2)}) collective-permute-start(bf16[512,1024]{1,0:T(8,128)(2,1)S(1)} %get-tuple-element.79), channel_id=1, source_target_pairs={{0,1},{1,0},{2,3},{3,2},{4,5},{5,4},{6,7},{7,6},{8,9},{9,8},{10,11... | collective-permute-start | bytes 3145736 | tf_op jit(solution)/shard_map/ppermute | solution.py:13
  116.7 11.2 %collective-permute-start.29 = (bf16[128,1024]{1,0:T(8,128)(2,1)S(1)}, bf16[128,1024]{1,0:T(8,128)(2,1)S(1)}, u32[]{:S(2)}, u32[]{:S(2)}) collective-permute-start(bf16[128,1024]{1,0:T(8,128)(2,1)S(1)} %get-tuple-element.49), channel_id=1, source_target_pairs={{0,6},{1,7},{2,4},{3,5},{4,2},{5,3},{6,0},{7,1},{8,14},{9,15},{10,... | collective-permute-start | bytes 786440 | tf_op jit(solution)/shard_map/ppermute | solution.py:13
  119.5 33.6 %collective-permute-start.28 = (bf16[128,1024]{1,0:T(8,128)(2,1)S(1)}, bf16[128,1024]{1,0:T(8,128)(2,1)S(1)}, u32[]{:S(2)}, u32[]{:S(2)}) collective-permute-start(bf16[128,1024]{1,0:T(8,128)(2,1)S(1)} %get-tuple-element.50), channel_id=1, source_target_pairs={{0,4},{1,5},{2,6},{3,7},{4,0},{5,1},{6,2},{7,3},{8,12},{9,13},{10,... | collective-permute-start | bytes 786440 | tf_op jit(solution)/shard_map/ppermute | solution.py:13
  119.5 33.6 %collective-permute-start.27 = (bf16[128,1024]{1,0:T(8,128)(2,1)S(1)}, bf16[128,1024]{1,0:T(8,128)(2,1)S(1)}, u32[]{:S(2)}, u32[]{:S(2)}) collective-permute-start(bf16[128,1024]{1,0:T(8,128)(2,1)S(1)} %get-tuple-element.48), channel_id=1, source_target_pairs={{0,2},{1,3},{2,0},{3,1},{4,6},{5,7},{6,4},{7,5},{8,10},{9,11},{10,... | collective-permute-start | bytes 786440 | tf_op jit(solution)/shard_map/ppermute | solution.py:13
  121.6 32.4 %collective-permute-start.20 = (bf16[128,1024]{1,0:T(8,128)(2,1)S(1)}, bf16[128,1024]{1,0:T(8,128)(2,1)S(1)}, u32[]{:S(2)}, u32[]{:S(2)}) collective-permute-start(bf16[128,1024]{1,0:T(8,128)(2,1)S(1)} %get-tuple-element.52), channel_id=1, source_target_pairs={{0,6},{1,7},{2,4},{3,5},{4,2},{5,3},{6,0},{7,1},{8,14},{9,15},{10,... | collective-permute-start | bytes 786440 | tf_op jit(solution)/shard_map/ppermute | solution.py:13
  124.4 39.5 %collective-permute-start.19 = (bf16[128,1024]{1,0:T(8,128)(2,1)S(1)}, bf16[128,1024]{1,0:T(8,128)(2,1)S(1)}, u32[]{:S(2)}, u32[]{:S(2)}) collective-permute-start(bf16[128,1024]{1,0:T(8,128)(2,1)S(1)} %get-tuple-element.53), channel_id=1, source_target_pairs={{0,4},{1,5},{2,6},{3,7},{4,0},{5,1},{6,2},{7,3},{8,12},{9,13},{10,... | collective-permute-start | bytes 786440 | tf_op jit(solution)/shard_map/ppermute | solution.py:13
  127.9 36.0 %collective-permute-start.18 = (bf16[128,1024]{1,0:T(8,128)(2,1)S(1)}, bf16[128,1024]{1,0:T(8,128)(2,1)S(1)}, u32[]{:S(2)}, u32[]{:S(2)}) collective-permute-start(bf16[128,1024]{1,0:T(8,128)(2,1)S(1)} %get-tuple-element.51), channel_id=1, source_target_pairs={{0,2},{1,3},{2,0},{3,1},{4,6},{5,7},{6,4},{7,5},{8,10},{9,11},{10,... | collective-permute-start | bytes 786440 | tf_op jit(solution)/shard_map/ppermute | solution.py:13

commit v2 on v1

--- a/solution.py
+++ b/solution.py
@@ -151,7 +151,7 @@
     o0, g0 = backward(c0, p0, q0)
     o1, g1 = backward(c1, p1, q1)
     b1, b0 = rowgrad(g1), rowgrad(g0)
-    t0, r0, t1, r1, _ = lax.optimization_barrier((c0, r0, c1, r1, b0))
+    t0, r0, t1, r1, _ = lax.optimization_barrier((c0, r0, c1, r1, g1))
     i0 = jnp.sum(t0.astype(F32) * r0.astype(F32), axis=1)
     i1 = jnp.sum(t1.astype(F32) * r1.astype(F32), axis=1)
     input_grad = shuffle(collect(b0, b1, rows))
@@ -160,9 +160,12 @@
     down_parts = [down_part[j * dhid : (j + 1) * dhid] for j in range(data_devices)]
     down_parts = in_order(down_parts, own)
     down_grad = scatter_rows(down_parts)
-    gu_part = mm(x0, g0, ((0,), (0,))) + mm(x1, g1, ((0,), (0,)))
-    gu_part = (gu_part * scale).astype(BF)
-    gu_grad = scatter_rows([gu_part[j * dwidth : (j + 1) * dwidth] for j in range(data_devices)])
+    gu_parts = []
+    for m in range(data_devices):
+        cols = slice(m * dwidth, (m + 1) * dwidth)
+        part = mm(x0[:, cols], g0, ((0,), (0,))) + mm(x1[:, cols], g1, ((0,), (0,)))
+        gu_parts.append(lax.optimization_barrier((part * scale).astype(BF)))
+    gu_grad = scatter_rows(gu_parts)
 
     mine = i0.reshape(pairs, rows)
     other = send(i1.reshape(pairs, rows), "expert", 1)

time: 165 us -> 164 us (level)
  waiting for transfers between devices: 79.3 us -> 77.6 us
    ppermute x40, waiting for transfers between devices: 79.3 us -> 77.6 us  [send(): return lax.ppermute(x, axis, pairs)]
    dot_general x12 -> x18, matrix products: 13 us -> 14.1 us  [mm(): lax.dot_general(a, b, ((dims[0], dims[1]), ((), ())), preferred_element_t...]
  transfers between devices with their start and end apart: 40 -> 40, of which waited for: 16 -> 15; matrix products, arithmetic and copies ran while one was open for 13% -> 13% of each run, Pallas kernels for 0% -> 0%
where the time goes in v2:
time: 164 us
  waiting for transfers between devices  77.6 us (47%)
  starting transfers between devices  59.3 us (36%)
  matrix products  14.1 us (9%)
  other arithmetic  10.8 us (7%)
    ppermute x40, waiting for transfers between devices, send(): return lax.ppermute(x, axis, pairs)  77.6 us
    ppermute x40, starting transfers between devices, send(): return lax.ppermute(x, axis, pairs)  59.3 us
    dot_general x18, matrix products, mm(): lax.dot_general(a, b, ((dims[0], dims[1]), ((), ())), preferred_element_t...  14.1 us
  transfers between devices with their start and end apart: 40, of which 15 were waited for; matrix products, arithmetic and copies ran while one was open for 13% of the time, Pallas kernels for 0%

profile of v2, /device:TPU:0, one launch (start us, length us, event | category | flops | bytes accessed | tf_op | source)
XLA Modules:
  0.0 164.1 jit_solution(10554945313140266120)
XLA Ops:
  0.7 0.8 select_reduce_fusion
  1.4 5.1 %collective-permute-start.2 = (f32[8,128]{1,0:T(8,128)S(1)}, f32[8,128]{1,0:T(8,128)S(1)}, u32[]{:S(2)}, u32[]{:S(2)}) collective-permute-start(f32[8,128]{1,0:T(8,128)S(1)} %select_reduce_fusion), channel_id=1, source_target_pairs={{0,6},{1,7},{2,4},{3,5},{4,2},{5,3},{6,0},{7,1},{8,14},{9,15},{10,... | collective-permute-start | bytes 12296 | tf_op jit(solution)/shard_map/ppermute | solution.py:13
  6.5 0.6 collective-permute-start
  7.1 1.0 broadcast_select_fusion.32
  8.1 0.7 collective-permute-start.5
  8.8 4.2 %collective-permute-start.4 = (bf16[128,1024]{1,0:T(8,128)(2,1)S(1)}, bf16[128,1024]{1,0:T(8,128)(2,1)S(1)}, u32[]{:S(2)}, u32[]{:S(2)}) collective-permute-start(bf16[128,1024]{1,0:T(8,128)(2,1)S(1)} %pad_maximum_fusion.6), channel_id=1, source_target_pairs={{0,4},{1,5},{2,6},{3,7},{4,0},{5,1},{6,2},{7,3},{8,12},{9,13},{10,... | collective-permute-start | bytes 786440 | tf_op jit(solution)/shard_map/ppermute | solution.py:13
  13.0 2.0 %pad_maximum_fusion.5 = (bf16[256,1024]{1,0:T(8,128)(2,1)S(1)}, bf16[1024,1024]{1,0:T(8,128)(2,1)}) fusion(bf16[256,512]{1,0:T(8,128)(2,1)} %bitcast.78, bf16[256,512]{1,0:T(8,128)(2,1)} %bitcast.79), kind=kLoop, calls=%fused_computation.41 | loop fusion | flops 1048575 | bytes 1572864 | tf_op jit(solution)/shard_map/concatenate | solution.py:109
  14.9 1.5 collective-permute-start.11
  16.4 1.5 collective-permute-start.13
  18.0 3.9 %collective-permute-done.11 = bf16[128,1024]{1,0:T(8,128)(2,1)S(1)} collective-permute-done((bf16[128,1024]{1,0:T(8,128)(2,1)S(1)}, bf16[128,1024]{1,0:T(8,128)(2,1)S(1)}, u32[]{:S(2)}, u32[]{:S(2)}) %collective-permute-start.11) | collective-permute-done | bytes 262176 | tf_op jit(solution)/shard_map/ppermute | solution.py:13
  22.2 1.6 collective-permute-start.12
  23.8 1.6 collective-permute-start.14
  25.4 2.1 %collective-permute-done.12 = bf16[64,1024]{1,0:T(8,128)(2,1)S(1)} collective-permute-done((bf16[64,1024]{1,0:T(8,128)(2,1)S(1)}, bf16[64,1024]{1,0:T(8,128)(2,1)S(1)}, u32[]{:S(2)}, u32[]{:S(2)}) %collective-permute-start.12) | collective-permute-done | bytes 131104 | tf_op jit(solution)/shard_map/ppermute | solution.py:13
  27.5 1.5 collective-permute-start.7
  29.0 0.7 collective-permute-done.4
  29.7 2.4 %collective-permute-start.22 = (bf16[128,1024]{1,0:T(8,128)(2,1)S(1)}, bf16[128,1024]{1,0:T(8,128)(2,1)S(1)}, u32[]{:S(2)}, u32[]{:S(2)}) collective-permute-start(bf16[128,1024]{1,0:T(8,128)(2,1)S(1)} %copy-done.1), channel_id=1, source_target_pairs={{0,4},{1,5},{2,6},{3,7},{4,0},{5,1},{6,2},{7,3},{8,12},{9,13},{10,... | collective-permute-start | bytes 786440 | tf_op jit(solution)/shard_map/ppermute | solution.py:13
  32.1 1.3 collective-permute-start.6
  33.5 1.6 collective-permute-start.8
  35.2 7.7 %collective-permute-done.22 = bf16[128,1024]{1,0:T(8,128)(2,1)S(1)} collective-permute-done((bf16[128,1024]{1,0:T(8,128)(2,1)S(1)}, bf16[128,1024]{1,0:T(8,128)(2,1)S(1)}, u32[]{:S(2)}, u32[]{:S(2)}) %collective-permute-start.22) | collective-permute-done | bytes 262176 | tf_op jit(solution)/shard_map/ppermute | solution.py:13
  42.9 0.7 collective-permute-start.23
  43.5 1.6 collective-permute-done.6
  45.1 1.3 collective-permute-start.24
  46.5 2.7 %collective-permute-start.21 = (bf16[128,1024]{1,0:T(8,128)(2,1)S(1)}, bf16[128,1024]{1,0:T(8,128)(2,1)S(1)}, u32[]{:S(2)}, u32[]{:S(2)}) collective-permute-start(bf16[128,1024]{1,0:T(8,128)(2,1)S(1)} %copy-done.1), channel_id=1, source_target_pairs={{0,2},{1,3},{2,0},{3,1},{4,6},{5,7},{6,4},{7,5},{8,10},{9,11},{10,... | collective-permute-start | bytes 786440 | tf_op jit(solution)/shard_map/ppermute | solution.py:13
  49.4 1.3 collective-permute-start.9
  50.7 1.6 collective-permute-start.10
  52.3 3.9 %collective-permute-done.24 = bf16[128,1024]{1,0:T(8,128)(2,1)S(1)} collective-permute-done((bf16[128,1024]{1,0:T(8,128)(2,1)S(1)}, bf16[128,1024]{1,0:T(8,128)(2,1)S(1)}, u32[]{:S(2)}, u32[]{:S(2)}) %collective-permute-start.24) | collective-permute-done | bytes 262176 | tf_op jit(solution)/shard_map/ppermute | solution.py:13
  56.2 3.0 %collective-permute-done.21 = bf16[128,1024]{1,0:T(8,128)(2,1)S(1)} collective-permute-done((bf16[128,1024]{1,0:T(8,128)(2,1)S(1)}, bf16[128,1024]{1,0:T(8,128)(2,1)S(1)}, u32[]{:S(2)}, u32[]{:S(2)}) %collective-permute-start.21) | collective-permute-done | bytes 262176 | tf_op jit(solution)/shard_map/ppermute | solution.py:13
  59.7 1.3 fusion.26
  61.3 0.7 convolution_convert_fusion.3
  62.1 1.3 fusion.27
  63.7 0.7 multiply_convert_fusion.3
  64.4 1.0 multiply_convert_fusion.8
  65.6 0.5 fusion.12
  67.5 1.3 convolution_convert_fusion.1
  69.0 1.0 multiply_convert_fusion.6
  70.2 1.3 convolution_convert_fusion
  71.5 0.6 collective-permute-start.26
  73.3 2.5 %collective-permute-start.36 = (bf16[256,1024]{1,0:T(8,128)(2,1)S(1)}, bf16[256,1024]{1,0:T(8,128)(2,1)S(1)}, u32[]{:S(2)}, u32[]{:S(2)}) collective-permute-start(bf16[256,1024]{1,0:T(8,128)(2,1)S(1)} %fusion.7), channel_id=1, source_target_pairs={{0,24},{8,16},{16,8},{24,0},{1,25},{9,17},{17,9},{25,1},{2,26},{10... | collective-permute-start | bytes 1572872 | tf_op jit(solution)/shard_map/ppermute | solution.py:13
  75.8 0.9 fusion.28
  76.7 0.7 multiply_convert_fusion
  78.5 0.5 fusion.4
  79.0 0.5 collective-permute-start.39
  79.6 1.5 collective-permute-start.38
  81.1 2.7 %collective-permute-start.33 = (f32[2,128]{1,0:T(2,128)S(1)}, f32[2,128]{1,0:T(2,128)S(1)}, u32[]{:S(2)}, u32[]{:S(2)}) collective-permute-start(f32[2,128]{1,0:T(2,128)S(1)} %get-tuple-element.69), channel_id=1, source_target_pairs={{0,6},{1,7},{2,4},{3,5},{4,2},{5,3},{6,0},{7,1},{8,14},{9,15},{10,... | collective-permute-start | bytes 3080 | tf_op jit(solution)/shard_map/ppermute | solution.py:13
  83.9 2.7 %collective-permute-done.33 = f32[2,128]{1,0:T(2,128)S(1)} collective-permute-done((f32[2,128]{1,0:T(2,128)S(1)}, f32[2,128]{1,0:T(2,128)S(1)}, u32[]{:S(2)}, u32[]{:S(2)}) %collective-permute-start.33) | collective-permute-done | bytes 1056 | tf_op jit(solution)/shard_map/ppermute | solution.py:13
  86.6 4.5 %collective-permute-done.32 = f32[2,128]{1,0:T(2,128)S(1)} collective-permute-done((f32[2,128]{1,0:T(2,128)S(1)}, f32[2,128]{1,0:T(2,128)S(1)}, u32[]{:S(2)}, u32[]{:S(2)}) %collective-permute-start.32) | collective-permute-done | bytes 1056 | tf_op jit(solution)/shard_map/ppermute | solution.py:13
  91.4 3.2 %collective-permute-done.31 = f32[2,128]{1,0:T(2,128)S(1)} collective-permute-done((f32[2,128]{1,0:T(2,128)S(1)}, f32[2,128]{1,0:T(2,128)S(1)}, u32[]{:S(2)}, u32[]{:S(2)}) %collective-permute-start.31) | collective-permute-done | bytes 1056 | tf_op jit(solution)/shard_map/ppermute | solution.py:13
  94.6 0.5 collective-permute-start.35
  95.1 1.5 collective-permute-start.34
  96.6 3.4 %collective-permute-done.38 = bf16[128,1024]{1,0:T(8,128)(2,1)S(1)} collective-permute-done((bf16[128,1024]{1,0:T(8,128)(2,1)S(1)}, bf16[128,1024]{1,0:T(8,128)(2,1)S(1)}, u32[]{:S(2)}, u32[]{:S(2)}) %collective-permute-start.38) | collective-permute-done | bytes 262176 | tf_op jit(solution)/shard_map/ppermute | solution.py:13
  100.0 1.5 collective-permute-start.37
  101.4 0.6 select_add_fusion
  102.0 11.3 %collective-permute-done.37 = bf16[128,1024]{1,0:T(8,128)(2,1)S(1)} collective-permute-done((bf16[128,1024]{1,0:T(8,128)(2,1)S(1)}, bf16[128,1024]{1,0:T(8,128)(2,1)S(1)}, u32[]{:S(2)}, u32[]{:S(2)}) %collective-permute-start.37) | collective-permute-done | bytes 262176 | tf_op jit(solution)/shard_map/ppermute | solution.py:13
  113.4 1.0 fusion.10
  114.8 0.8 slice_bitcast_fusion
  116.1 2.7 %collective-permute-start.29 = (bf16[128,1024]{1,0:T(8,128)(2,1)S(1)}, bf16[128,1024]{1,0:T(8,128)(2,1)S(1)}, u32[]{:S(2)}, u32[]{:S(2)}) collective-permute-start(bf16[128,1024]{1,0:T(8,128)(2,1)S(1)} %get-tuple-element.46), channel_id=1, source_target_pairs={{0,6},{1,7},{2,4},{3,5},{4,2},{5,3},{6,0},{7,1},{8,14},{9,15},{10,... | collective-permute-start | bytes 786440 | tf_op jit(solution)/shard_map/ppermute | solution.py:13
  118.8 1.7 %collective-permute-start.27 = (bf16[128,1024]{1,0:T(8,128)(2,1)S(1)}, bf16[128,1024]{1,0:T(8,128)(2,1)S(1)}, u32[]{:S(2)}, u32[]{:S(2)}) collective-permute-start(bf16[128,1024]{1,0:T(8,128)(2,1)S(1)} %get-tuple-element.45), channel_id=1, source_target_pairs={{0,2},{1,3},{2,0},{3,1},{4,6},{5,7},{6,4},{7,5},{8,10},{9,11},{10,... | collective-permute-start | bytes 786440 | tf_op jit(solution)/shard_map/ppermute | solution.py:13
  121.0 2.7 %collective-permute-start.20 = (bf16[128,1024]{1,0:T(8,128)(2,1)S(1)}, bf16[128,1024]{1,0:T(8,128)(2,1)S(1)}, u32[]{:S(2)}, u32[]{:S(2)}) collective-permute-start(bf16[128,1024]{1,0:T(8,128)(2,1)S(1)} %get-tuple-element.49), channel_id=1, source_target_pairs={{0,6},{1,7},{2,4},{3,5},{4,2},{5,3},{6,0},{7,1},{8,14},{9,15},{10,... | collective-permute-start | bytes 786440 | tf_op jit(solution)/shard_map/ppermute | solution.py:13
  123.7 3.5 %collective-permute-done.29 = bf16[128,1024]{1,0:T(8,128)(2,1)S(1)} collective-permute-done((bf16[128,1024]{1,0:T(8,128)(2,1)S(1)}, bf16[128,1024]{1,0:T(8,128)(2,1)S(1)}, u32[]{:S(2)}, u32[]{:S(2)}) %collective-permute-start.29) | collective-permute-done | bytes 262176 | tf_op jit(solution)/shard_map/ppermute | solution.py:13
  127.3 8.8 %collective-permute-start.18 = (bf16[128,1024]{1,0:T(8,128)(2,1)S(1)}, bf16[128,1024]{1,0:T(8,128)(2,1)S(1)}, u32[]{:S(2)}, u32[]{:S(2)}) collective-permute-start(bf16[128,1024]{1,0:T(8,128)(2,1)S(1)} %get-tuple-element.48), channel_id=1, source_target_pairs={{0,2},{1,3},{2,0},{3,1},{4,6},{5,7},{6,4},{7,5},{8,10},{9,11},{10,... | collective-permute-start | bytes 786440 | tf_op jit(solution)/shard_map/ppermute | solution.py:13
  136.1 16.3 %collective-permute-done.28 = bf16[128,1024]{1,0:T(8,128)(2,1)S(1)} collective-permute-done((bf16[128,1024]{1,0:T(8,128)(2,1)S(1)}, bf16[128,1024]{1,0:T(8,128)(2,1)S(1)}, u32[]{:S(2)}, u32[]{:S(2)}) %collective-permute-start.28) | collective-permute-done | bytes 262176 | tf_op jit(solution)/shard_map/ppermute | solution.py:13
  152.6 0.7 pad_maximum_fusion.7
  153.4 9.9 %collective-permute-done.19 = bf16[128,1024]{1,0:T(8,128)(2,1)S(1)} collective-permute-done((bf16[128,1024]{1,0:T(8,128)(2,1)S(1)}, bf16[128,1024]{1,0:T(8,128)(2,1)S(1)}, u32[]{:S(2)}, u32[]{:S(2)}) %collective-permute-start.19) | collective-permute-done | bytes 262176 | tf_op jit(solution)/shard_map/ppermute | solution.py:13
  163.2 0.9 add_convert_fusion.5
  (94 shorter events, 8.0 us)
Async XLA Ops:
  0.6 14.3 %copy-start = (bf16[1,128,1024]{2,1,0:T(8,128)(2,1)S(1)}, bf16[1,128,1024]{2,1,0:T(8,128)(2,1)}, u32[]{:S(2)}) copy-start(bf16[1,128,1024]{2,1,0:T(8,128)(2,1)} %param.12) | copy-start | bytes 786436
  0.6 29.0 %copy-start.1 = (bf16[128,1024]{1,0:T(8,128)(2,1)S(1)}, bf16[128,1024]{1,0:T(8,128)(2,1)}, u32[]{:S(2)}) copy-start(bf16[128,1024]{1,0:T(8,128)(2,1)} %param.13) | copy-start | bytes 786436
  1.4 13.5 %collective-permute-start.2 = (f32[8,128]{1,0:T(8,128)S(1)}, f32[8,128]{1,0:T(8,128)S(1)}, u32[]{:S(2)}, u32[]{:S(2)}) collective-permute-start(f32[8,128]{1,0:T(8,128)S(1)} %select_reduce_fusion), channel_id=1, source_target_pairs={{0,6},{1,7},{2,4},{3,5},{4,2},{5,3},{6,0},{7,1},{8,14},{9,15},{10,... | collective-permute-start | bytes 12296 | tf_op jit(solution)/shard_map/ppermute | solution.py:13
  6.5 10.0 %collective-permute-start.1 = (f32[8,128]{1,0:T(8,128)S(1)}, f32[8,128]{1,0:T(8,128)S(1)}, u32[]{:S(2)}, u32[]{:S(2)}) collective-permute-start(f32[8,128]{1,0:T(8,128)S(1)} %select_reduce_fusion), channel_id=1, source_target_pairs={{0,4},{1,5},{2,6},{3,7},{4,0},{5,1},{6,2},{7,3},{8,12},{9,13},{10,... | collective-permute-start | bytes 12296 | tf_op jit(solution)/shard_map/ppermute | solution.py:13
  6.5 11.4 %collective-permute-start = (f32[8,128]{1,0:T(8,128)S(1)}, f32[8,128]{1,0:T(8,128)S(1)}, u32[]{:S(2)}, u32[]{:S(2)}) collective-permute-start(f32[8,128]{1,0:T(8,128)S(1)} %select_reduce_fusion), channel_id=1, source_target_pairs={{0,2},{1,3},{2,0},{3,1},{4,6},{5,7},{6,4},{7,5},{8,10},{9,11},{10,... | collective-permute-start | bytes 12296 | tf_op jit(solution)/shard_map/ppermute | solution.py:13
  8.1 25.4 %collective-permute-start.5 = (bf16[128,1024]{1,0:T(8,128)(2,1)S(1)}, bf16[128,1024]{1,0:T(8,128)(2,1)S(1)}, u32[]{:S(2)}, u32[]{:S(2)}) collective-permute-start(bf16[128,1024]{1,0:T(8,128)(2,1)S(1)} %pad_maximum_fusion.6), channel_id=1, source_target_pairs={{2,4},{3,5},{4,2},{5,3},{10,12},{11,13},{12,10},{13,11},{18,20},{1... | collective-permute-start | bytes 786440 | tf_op jit(solution)/shard_map/ppermute | solution.py:13
  8.8 20.9 %collective-permute-start.4 = (bf16[128,1024]{1,0:T(8,128)(2,1)S(1)}, bf16[128,1024]{1,0:T(8,128)(2,1)S(1)}, u32[]{:S(2)}, u32[]{:S(2)}) collective-permute-start(bf16[128,1024]{1,0:T(8,128)(2,1)S(1)} %pad_maximum_fusion.6), channel_id=1, source_target_pairs={{0,4},{1,5},{2,6},{3,7},{4,0},{5,1},{6,2},{7,3},{8,12},{9,13},{10,... | collective-permute-start | bytes 786440 | tf_op jit(solution)/shard_map/ppermute | solution.py:13
  14.9 6.9 %collective-permute-start.11 = (bf16[128,1024]{1,0:T(8,128)(2,1)S(1)}, bf16[128,1024]{1,0:T(8,128)(2,1)S(1)}, u32[]{:S(2)}, u32[]{:S(2)}) collective-permute-start(bf16[128,1024]{1,0:T(8,128)(2,1)S(1)} %bitcast.80), channel_id=1, source_target_pairs={{0,16},{8,24},{16,0},{24,8},{1,17},{9,25},{17,1},{25,9},{2,18},{10... | collective-permute-start | bytes 786440 | tf_op jit(solution)/shard_map/ppermute | solution.py:13
  16.4 7.3 %collective-permute-start.13 = (bf16[128,1024]{1,0:T(8,128)(2,1)S(1)}, bf16[128,1024]{1,0:T(8,128)(2,1)S(1)}, u32[]{:S(2)}, u32[]{:S(2)}) collective-permute-start(bf16[128,1024]{1,0:T(8,128)(2,1)S(1)} %bitcast.81), channel_id=1, source_target_pairs={{0,8},{8,0},{16,24},{24,16},{1,9},{9,1},{17,25},{25,17},{2,10},{10... | collective-permute-start | bytes 786440 | tf_op jit(solution)/shard_map/ppermute | solution.py:13
  17.9 4.2 %collective-permute-start.15 = (f32[4,8,128]{2,1,0:T(8,128)S(1)}, f32[4,8,128]{2,1,0:T(8,128)S(1)}, u32[]{:S(2)}, u32[]{:S(2)}) collective-permute-start(f32[4,8,128]{2,1,0:T(8,128)S(1)} %pad_maximum_fusion.8), channel_id=1, source_target_pairs={{0,1},{1,0},{2,3},{3,2},{4,5},{5,4},{6,7},{7,6},{8,9},{9,8},{10,11... | collective-permute-start | bytes 49160 | tf_op jit(solution)/shard_map/ppermute | solution.py:13
  21.9 24.6 %collective-permute-start.3 = (bf16[128,1024]{1,0:T(8,128)(2,1)S(1)}, bf16[128,1024]{1,0:T(8,128)(2,1)S(1)}, u32[]{:S(2)}, u32[]{:S(2)}) collective-permute-start(bf16[128,1024]{1,0:T(8,128)(2,1)S(1)} %pad_maximum_fusion.6), channel_id=1, source_target_pairs={{0,2},{1,3},{2,0},{3,1},{4,6},{5,7},{6,4},{7,5},{8,10},{9,11},{10,... | collective-permute-start | bytes 786440 | tf_op jit(solution)/shard_map/ppermute | solution.py:13
  22.2 5.3 %collective-permute-start.12 = (bf16[64,1024]{1,0:T(8,128)(2,1)S(1)}, bf16[64,1024]{1,0:T(8,128)(2,1)S(1)}, u32[]{:S(2)}, u32[]{:S(2)}) collective-permute-start(bf16[64,1024]{1,0:T(8,128)(2,1)S(1)} %slice.225), channel_id=1, source_target_pairs={{0,8},{8,0},{16,24},{24,16},{1,9},{9,1},{17,25},{25,17},{2,10},{10... | collective-permute-start | bytes 393224 | tf_op jit(solution)/shard_map/ppermute | solution.py:13
  23.8 8.3 %collective-permute-start.14 = (bf16[64,1024]{1,0:T(8,128)(2,1)S(1)}, bf16[64,1024]{1,0:T(8,128)(2,1)S(1)}, u32[]{:S(2)}, u32[]{:S(2)}) collective-permute-start(bf16[64,1024]{1,0:T(8,128)(2,1)S(1)} %slice.226), channel_id=1, source_target_pairs={{0,16},{8,24},{16,0},{24,8},{1,17},{9,25},{17,1},{25,9},{2,18},{10... | collective-permute-start | bytes 393224 | tf_op jit(solution)/shard_map/ppermute | solution.py:13
  27.5 21.9 %collective-permute-start.7 = (bf16[256,1024]{1,0:T(8,128)(2,1)S(1)}, bf16[256,1024]{1,0:T(8,128)(2,1)S(1)}, u32[]{:S(2)}, u32[]{:S(2)}) collective-permute-start(bf16[256,1024]{1,0:T(8,128)(2,1)S(1)} %get-tuple-element.57), channel_id=1, source_target_pairs={{0,8},{8,0},{16,24},{24,16},{1,9},{9,1},{17,25},{25,17},{2,10},{10... | collective-permute-start | bytes 1572872 | tf_op jit(solution)/shard_map/ppermute | solution.py:13
  29.7 13.2 %collective-permute-start.22 = (bf16[128,1024]{1,0:T(8,128)(2,1)S(1)}, bf16[128,1024]{1,0:T(8,128)(2,1)S(1)}, u32[]{:S(2)}, u32[]{:S(2)}) collective-permute-start(bf16[128,1024]{1,0:T(8,128)(2,1)S(1)} %copy-done.1), channel_id=1, source_target_pairs={{0,4},{1,5},{2,6},{3,7},{4,0},{5,1},{6,2},{7,3},{8,12},{9,13},{10,... | collective-permute-start | bytes 786440 | tf_op jit(solution)/shard_map/ppermute | solution.py:13
  32.1 13.0 %collective-permute-start.6 = (bf16[128,1024]{1,0:T(8,128)(2,1)S(1)}, bf16[128,1024]{1,0:T(8,128)(2,1)S(1)}, u32[]{:S(2)}, u32[]{:S(2)}) collective-permute-start(bf16[128,1024]{1,0:T(8,128)(2,1)S(1)} %collective-permute-done.4), channel_id=1, source_target_pairs={{2,0},{3,1},{4,6},{5,7},{10,8},{11,9},{12,14},{13,15},{18,16},{19,... | collective-permute-start | bytes 786440 | tf_op jit(solution)/shard_map/ppermute | solution.py:13
  33.5 15.7 %collective-permute-start.8 = (bf16[256,1024]{1,0:T(8,128)(2,1)S(1)}, bf16[256,1024]{1,0:T(8,128)(2,1)S(1)}, u32[]{:S(2)}, u32[]{:S(2)}) collective-permute-start(bf16[256,1024]{1,0:T(8,128)(2,1)S(1)} %get-tuple-element.57), channel_id=1, source_target_pairs={{0,16},{8,24},{16,0},{24,8},{1,17},{9,25},{17,1},{25,9},{2,18},{10... | collective-permute-start | bytes 1572872 | tf_op jit(solution)/shard_map/ppermute | solution.py:13
  42.9 7.9 %collective-permute-start.23 = (bf16[128,1024]{1,0:T(8,128)(2,1)S(1)}, bf16[128,1024]{1,0:T(8,128)(2,1)S(1)}, u32[]{:S(2)}, u32[]{:S(2)}) collective-permute-start(bf16[128,1024]{1,0:T(8,128)(2,1)S(1)} %copy-done.1), channel_id=1, source_target_pairs={{2,4},{3,5},{4,2},{5,3},{10,12},{11,13},{12,10},{13,11},{18,20},{1... | collective-permute-start | bytes 786440 | tf_op jit(solution)/shard_map/ppermute | solution.py:13
  45.1 11.1 %collective-permute-start.24 = (bf16[128,1024]{1,0:T(8,128)(2,1)S(1)}, bf16[128,1024]{1,0:T(8,128)(2,1)S(1)}, u32[]{:S(2)}, u32[]{:S(2)}) collective-permute-start(bf16[128,1024]{1,0:T(8,128)(2,1)S(1)} %collective-permute-done.22), channel_id=1, source_target_pairs={{2,0},{3,1},{4,6},{5,7},{10,8},{11,9},{12,14},{13,15},{18,16},{19,... | collective-permute-start | bytes 786440 | tf_op jit(solution)/shard_map/ppermute | solution.py:13
  46.5 12.7 %collective-permute-start.21 = (bf16[128,1024]{1,0:T(8,128)(2,1)S(1)}, bf16[128,1024]{1,0:T(8,128)(2,1)S(1)}, u32[]{:S(2)}, u32[]{:S(2)}) collective-permute-start(bf16[128,1024]{1,0:T(8,128)(2,1)S(1)} %copy-done.1), channel_id=1, source_target_pairs={{0,2},{1,3},{2,0},{3,1},{4,6},{5,7},{6,4},{7,5},{8,10},{9,11},{10,... | collective-permute-start | bytes 786440 | tf_op jit(solution)/shard_map/ppermute | solution.py:13
  49.3 12.8 %collective-permute-start.16 = (bf16[512,1024]{1,0:T(8,128)(2,1)S(1)}, bf16[512,1024]{1,0:T(8,128)(2,1)S(1)}, u32[]{:S(2)}, u32[]{:S(2)}) collective-permute-start(bf16[512,1024]{1,0:T(8,128)(2,1)S(1)} %pad_maximum_fusion), channel_id=1, source_target_pairs={{0,1},{1,0},{2,3},{3,2},{4,5},{5,4},{6,7},{7,6},{8,9},{9,8},{10,11... | collective-permute-start | bytes 3145736 | tf_op jit(solution)/shard_map/ppermute | solution.py:13
  49.4 10.3 %collective-permute-start.9 = (bf16[128,1024]{1,0:T(8,128)(2,1)S(1)}, bf16[128,1024]{1,0:T(8,128)(2,1)S(1)}, u32[]{:S(2)}, u32[]{:S(2)}) collective-permute-start(bf16[128,1024]{1,0:T(8,128)(2,1)S(1)} %slice.221), channel_id=1, source_target_pairs={{0,8},{8,0},{16,24},{24,16},{1,9},{9,1},{17,25},{25,17},{2,10},{10... | collective-permute-start | bytes 786440 | tf_op jit(solution)/shard_map/ppermute | solution.py:13
  50.7 9.0 %collective-permute-start.10 = (bf16[128,1024]{1,0:T(8,128)(2,1)S(1)}, bf16[128,1024]{1,0:T(8,128)(2,1)S(1)}, u32[]{:S(2)}, u32[]{:S(2)}) collective-permute-start(bf16[128,1024]{1,0:T(8,128)(2,1)S(1)} %slice.222), channel_id=1, source_target_pairs={{0,16},{8,24},{16,0},{24,8},{1,17},{9,25},{17,1},{25,9},{2,18},{10... | collective-permute-start | bytes 786440 | tf_op jit(solution)/shard_map/ppermute | solution.py:13
  56.2 3.4 %copy-start.2 = (bf16[1024,1024]{1,0:T(8,128)(2,1)S(1)}, bf16[1024,1024]{1,0:T(8,128)(2,1)}, u32[]{:S(2)}) copy-start(bf16[1024,1024]{1,0:T(8,128)(2,1)} %get-tuple-element.58) | copy-start | bytes 6291460
  59.2 9.5 %collective-permute-start.25 = (bf16[512,1024]{1,0:T(8,128)(2,1)S(1)}, bf16[512,1024]{1,0:T(8,128)(2,1)S(1)}, u32[]{:S(2)}, u32[]{:S(2)}) collective-permute-start(bf16[512,1024]{1,0:T(8,128)(2,1)S(1)} %pad_maximum_fusion.2), channel_id=1, source_target_pairs={{0,1},{1,0},{2,3},{3,2},{4,5},{5,4},{6,7},{7,6},{8,9},{9,8},{10,11... | collective-permute-start | bytes 3145736 | tf_op jit(solution)/shard_map/ppermute | solution.py:13
  71.5 44.1 %collective-permute-start.26 = (bf16[512,1024]{1,0:T(8,128)(2,1)S(1)}, bf16[512,1024]{1,0:T(8,128)(2,1)S(1)}, u32[]{:S(2)}, u32[]{:S(2)}) collective-permute-start(bf16[512,1024]{1,0:T(8,128)(2,1)S(1)} %convolution_convert_fusion), channel_id=1, source_target_pairs={{0,1},{1,0},{2,3},{3,2},{4,5},{5,4},{6,7},{7,6},{8,9},{9,8},{10,11... | collective-permute-start | bytes 3145736 | tf_op jit(solution)/shard_map/ppermute | solution.py:13
  72.4 8.7 %collective-permute-start.30 = (f32[4,128]{1,0:T(4,128)S(1)}, f32[4,128]{1,0:T(4,128)S(1)}, u32[]{:S(2)}, u32[]{:S(2)}) collective-permute-start(f32[4,128]{1,0:T(4,128)S(1)} %bitcast.92), channel_id=1, source_target_pairs={{0,1},{1,0},{2,3},{3,2},{4,5},{5,4},{6,7},{7,6},{8,9},{9,8},{10,11... | collective-permute-start | bytes 6152 | tf_op jit(solution)/shard_map/ppermute | solution.py:13
  73.3 41.0 %collective-permute-start.36 = (bf16[256,1024]{1,0:T(8,128)(2,1)S(1)}, bf16[256,1024]{1,0:T(8,128)(2,1)S(1)}, u32[]{:S(2)}, u32[]{:S(2)}) collective-permute-start(bf16[256,1024]{1,0:T(8,128)(2,1)S(1)} %fusion.7), channel_id=1, source_target_pairs={{0,24},{8,16},{16,8},{24,0},{1,25},{9,17},{17,9},{25,1},{2,26},{10... | collective-permute-start | bytes 1572872 | tf_op jit(solution)/shard_map/ppermute | solution.py:13
  78.5 23.0 %copy-start.3 = (s32[128,4]{0,1:T(4,128)S(1)}, s32[128,4]{0,1:T(4,128)}, u32[]{:S(2)}) copy-start(s32[128,4]{0,1:T(4,128)} %param.8) | copy-start | bytes 6148
  79.0 16.1 %collective-permute-start.39 = (bf16[128,1024]{1,0:T(8,128)(2,1)S(1)}, bf16[128,1024]{1,0:T(8,128)(2,1)S(1)}, u32[]{:S(2)}, u32[]{:S(2)}) collective-permute-start(bf16[128,1024]{1,0:T(8,128)(2,1)S(1)} %get-tuple-element.44), channel_id=1, source_target_pairs={{0,24},{8,16},{16,8},{24,0},{1,25},{9,17},{17,9},{25,1},{2,26},{10... | collective-permute-start | bytes 786440 | tf_op jit(solution)/shard_map/ppermute | solution.py:13
  79.6 20.4 %collective-permute-start.38 = (bf16[128,1024]{1,0:T(8,128)(2,1)S(1)}, bf16[128,1024]{1,0:T(8,128)(2,1)S(1)}, u32[]{:S(2)}, u32[]{:S(2)}) collective-permute-start(bf16[128,1024]{1,0:T(8,128)(2,1)S(1)} %get-tuple-element.43), channel_id=1, source_target_pairs={{0,16},{8,24},{16,0},{24,8},{1,17},{9,25},{17,1},{25,9},{2,18},{10... | collective-permute-start | bytes 786440 | tf_op jit(solution)/shard_map/ppermute | solution.py:13
  81.1 5.4 %collective-permute-start.33 = (f32[2,128]{1,0:T(2,128)S(1)}, f32[2,128]{1,0:T(2,128)S(1)}, u32[]{:S(2)}, u32[]{:S(2)}) collective-permute-start(f32[2,128]{1,0:T(2,128)S(1)} %get-tuple-element.69), channel_id=1, source_target_pairs={{0,6},{1,7},{2,4},{3,5},{4,2},{5,3},{6,0},{7,1},{8,14},{9,15},{10,... | collective-permute-start | bytes 3080 | tf_op jit(solution)/shard_map/ppermute | solution.py:13
  86.5 4.5 %collective-permute-start.32 = (f32[2,128]{1,0:T(2,128)S(1)}, f32[2,128]{1,0:T(2,128)S(1)}, u32[]{:S(2)}, u32[]{:S(2)}) collective-permute-start(f32[2,128]{1,0:T(2,128)S(1)} %get-tuple-element.68), channel_id=1, source_target_pairs={{0,4},{1,5},{2,6},{3,7},{4,0},{5,1},{6,2},{7,3},{8,12},{9,13},{10,... | collective-permute-start | bytes 3080 | tf_op jit(solution)/shard_map/ppermute | solution.py:13
  91.0 3.6 %collective-permute-start.31 = (f32[2,128]{1,0:T(2,128)S(1)}, f32[2,128]{1,0:T(2,128)S(1)}, u32[]{:S(2)}, u32[]{:S(2)}) collective-permute-start(f32[2,128]{1,0:T(2,128)S(1)} %get-tuple-element.67), channel_id=1, source_target_pairs={{0,2},{1,3},{2,0},{3,1},{4,6},{5,7},{6,4},{7,5},{8,10},{9,11},{10,... | collective-permute-start | bytes 3080 | tf_op jit(solution)/shard_map/ppermute | solution.py:13
  94.6 19.8 %collective-permute-start.35 = (bf16[256,1024]{1,0:T(8,128)(2,1)S(1)}, bf16[256,1024]{1,0:T(8,128)(2,1)S(1)}, u32[]{:S(2)}, u32[]{:S(2)}) collective-permute-start(bf16[256,1024]{1,0:T(8,128)(2,1)S(1)} %fusion.6), channel_id=1, source_target_pairs={{0,16},{8,24},{16,0},{24,8},{1,17},{9,25},{17,1},{25,9},{2,18},{10... | collective-permute-start | bytes 1572872 | tf_op jit(solution)/shard_map/ppermute | solution.py:13
  95.1 19.3 %collective-permute-start.34 = (bf16[256,1024]{1,0:T(8,128)(2,1)S(1)}, bf16[256,1024]{1,0:T(8,128)(2,1)S(1)}, u32[]{:S(2)}, u32[]{:S(2)}) collective-permute-start(bf16[256,1024]{1,0:T(8,128)(2,1)S(1)} %fusion.5), channel_id=1, source_target_pairs={{0,8},{8,0},{16,24},{24,16},{1,9},{9,1},{17,25},{25,17},{2,10},{10... | collective-permute-start | bytes 1572872 | tf_op jit(solution)/shard_map/ppermute | solution.py:13
  100.0 13.4 %collective-permute-start.37 = (bf16[128,1024]{1,0:T(8,128)(2,1)S(1)}, bf16[128,1024]{1,0:T(8,128)(2,1)S(1)}, u32[]{:S(2)}, u32[]{:S(2)}) collective-permute-start(bf16[128,1024]{1,0:T(8,128)(2,1)S(1)} %get-tuple-element.42), channel_id=1, source_target_pairs={{0,8},{8,0},{16,24},{24,16},{1,9},{9,1},{17,25},{25,17},{2,10},{10... | collective-permute-start | bytes 786440 | tf_op jit(solution)/shard_map/ppermute | solution.py:13
  113.4 7.2 %collective-permute-start.17 = (bf16[512,1024]{1,0:T(8,128)(2,1)S(1)}, bf16[512,1024]{1,0:T(8,128)(2,1)S(1)}, u32[]{:S(2)}, u32[]{:S(2)}) collective-permute-start(bf16[512,1024]{1,0:T(8,128)(2,1)S(1)} %get-tuple-element.76), channel_id=1, source_target_pairs={{0,1},{1,0},{2,3},{3,2},{4,5},{5,4},{6,7},{7,6},{8,9},{9,8},{10,11... | collective-permute-start | bytes 3145736 | tf_op jit(solution)/shard_map/ppermute | solution.py:13
  116.1 11.2 %collective-permute-start.29 = (bf16[128,1024]{1,0:T(8,128)(2,1)S(1)}, bf16[128,1024]{1,0:T(8,128)(2,1)S(1)}, u32[]{:S(2)}, u32[]{:S(2)}) collective-permute-start(bf16[128,1024]{1,0:T(8,128)(2,1)S(1)} %get-tuple-element.46), channel_id=1, source_target_pairs={{0,6},{1,7},{2,4},{3,5},{4,2},{5,3},{6,0},{7,1},{8,14},{9,15},{10,... | collective-permute-start | bytes 786440 | tf_op jit(solution)/shard_map/ppermute | solution.py:13
  118.8 33.6 %collective-permute-start.28 = (bf16[128,1024]{1,0:T(8,128)(2,1)S(1)}, bf16[128,1024]{1,0:T(8,128)(2,1)S(1)}, u32[]{:S(2)}, u32[]{:S(2)}) collective-permute-start(bf16[128,1024]{1,0:T(8,128)(2,1)S(1)} %get-tuple-element.47), channel_id=1, source_target_pairs={{0,4},{1,5},{2,6},{3,7},{4,0},{5,1},{6,2},{7,3},{8,12},{9,13},{10,... | collective-permute-start | bytes 786440 | tf_op jit(solution)/shard_map/ppermute | solution.py:13
  118.8 33.6 %collective-permute-start.27 = (bf16[128,1024]{1,0:T(8,128)(2,1)S(1)}, bf16[128,1024]{1,0:T(8,128)(2,1)S(1)}, u32[]{:S(2)}, u32[]{:S(2)}) collective-permute-start(bf16[128,1024]{1,0:T(8,128)(2,1)S(1)} %get-tuple-element.45), channel_id=1, source_target_pairs={{0,2},{1,3},{2,0},{3,1},{4,6},{5,7},{6,4},{7,5},{8,10},{9,11},{10,... | collective-permute-start | bytes 786440 | tf_op jit(solution)/shard_map/ppermute | solution.py:13
  121.0 32.4 %collective-permute-start.20 = (bf16[128,1024]{1,0:T(8,128)(2,1)S(1)}, bf16[128,1024]{1,0:T(8,128)(2,1)S(1)}, u32[]{:S(2)}, u32[]{:S(2)}) collective-permute-start(bf16[128,1024]{1,0:T(8,128)(2,1)S(1)} %get-tuple-element.49), channel_id=1, source_target_pairs={{0,6},{1,7},{2,4},{3,5},{4,2},{5,3},{6,0},{7,1},{8,14},{9,15},{10,... | collective-permute-start | bytes 786440 | tf_op jit(solution)/shard_map/ppermute | solution.py:13
  123.7 39.5 %collective-permute-start.19 = (bf16[128,1024]{1,0:T(8,128)(2,1)S(1)}, bf16[128,1024]{1,0:T(8,128)(2,1)S(1)}, u32[]{:S(2)}, u32[]{:S(2)}) collective-permute-start(bf16[128,1024]{1,0:T(8,128)(2,1)S(1)} %get-tuple-element.50), channel_id=1, source_target_pairs={{0,4},{1,5},{2,6},{3,7},{4,0},{5,1},{6,2},{7,3},{8,12},{9,13},{10,... | collective-permute-start | bytes 786440 | tf_op jit(solution)/shard_map/ppermute | solution.py:13
  127.3 36.0 %collective-permute-start.18 = (bf16[128,1024]{1,0:T(8,128)(2,1)S(1)}, bf16[128,1024]{1,0:T(8,128)(2,1)S(1)}, u32[]{:S(2)}, u32[]{:S(2)}) collective-permute-start(bf16[128,1024]{1,0:T(8,128)(2,1)S(1)} %get-tuple-element.48), channel_id=1, source_target_pairs={{0,2},{1,3},{2,0},{3,1},{4,6},{5,7},{6,4},{7,5},{8,10},{9,11},{10,... | collective-permute-start | bytes 786440 | tf_op jit(solution)/shard_map/ppermute | solution.py:13

commit v3 on v2

--- a/solution.py
+++ b/solution.py
@@ -13,33 +13,42 @@
     return lax.ppermute(x, axis, pairs)
 
 
-def spread(block):
+def block_order(pairs):
+    order, step = [0], pairs // 2
+    while step:
+        order, step = order + [a ^ step for a in order], step // 2
+    return order
+
+
+def spread(block, arrange=lambda x: x):
     pairs = lax.axis_size("expert") // 2
     if pairs == 4:
         inner = lambda a, b: a // 2 in (1, 2)
         two = send(block, "expert", 4)
         one = send(block, "expert", 2)
         mid = send(block, "expert", 6, inner)
-        far = send(two, "expert", 2, lambda a, b: a // 2 in (1, 2))
+        far = send(two, "expert", 2, inner)
         row = lax.axis_index("expert") // 2
         three = jnp.where((row == 1) | (row == 2), mid, far)
-        mine = [block, one, two, three]
+        mine = [block, two, one, three]
     else:
-        mine = [block] + [send(block, "expert", 2 * m) for m in range(1, pairs)]
-    mine = lax.optimization_barrier(jnp.concatenate(mine, axis=0))
+        mine = [block] + [send(block, "expert", 2 * m) for m in block_order(pairs)[1:]]
+    mine = lax.optimization_barrier(arrange(jnp.concatenate(mine, axis=0)))
     return mine, send(mine, "expert", 1)
 
 
-def collect(mine, other, rows):
+def collect(mine, other):
     pairs = lax.axis_size("expert") // 2
     got = send(other, "expert", 1)
     total = (mine.astype(F32) + got.astype(F32)).astype(BF)
     total = lax.optimization_barrier(total)
-    parts = [total[m * rows : (m + 1) * rows] for m in range(pairs)]
-    out = parts[0].astype(F32)
-    for m in range(1, pairs):
-        out = out + send(parts[m], "expert", 2 * m).astype(F32)
-    return out.astype(BF)
+    step = 1
+    while step < pairs:
+        half = total.shape[0] // 2
+        got = send(total[half:], "expert", 2 * step)
+        total = (total[:half].astype(F32) + got.astype(F32)).astype(BF)
+        step *= 2
+    return total
 
 
 def in_order(parts, own):
@@ -105,7 +114,7 @@
 
     chosen = expert_ids.T[None, :, :] == jnp.arange(experts, dtype=jnp.int32)[:, None, None]
     dense = jnp.sum(jnp.where(chosen, gate_probs.T[None, :, :], 0.0), axis=1)
-    x0, x1 = spread(shuffle(tokens))
+    x0, x1 = spread(tokens, shuffle)
     pair = jnp.concatenate([w_gate[0], w_up[0]], axis=1)
     wgu = gather_rows(pair)
     wgu = lax.optimization_barrier(jnp.concatenate(wgu, axis=0))
@@ -113,7 +122,7 @@
     wd = lax.optimization_barrier(jnp.concatenate(in_order(wd, own), axis=0))
     c0, c1 = spread(cotangent)
     near = [dense]
-    for m in range(1, pairs):
+    for m in block_order(pairs)[1:]:
         near.append(send(dense, "expert", 2 * m))
     near = lax.optimization_barrier(jnp.stack(near))
     far = send(near, "expert", 1)
@@ -145,7 +154,7 @@
     q0, q1 = project(x0), project(x1)
     h1, r1, m1 = forward(q1, p1)
     h0, r0, m0 = forward(q0, p0)
-    mixed = collect(m0, m1, rows)
+    mixed = collect(m0, m1)
     q0, h0, r0, q1, h1, r1 = lax.optimization_barrier((q0, h0, r0, q1, h1, r1))
     p0, p1 = lax.optimization_barrier((p0, p1))
     o0, g0 = backward(c0, p0, q0)
@@ -154,7 +163,7 @@
     t0, r0, t1, r1, _ = lax.optimization_barrier((c0, r0, c1, r1, g1))
     i0 = jnp.sum(t0.astype(F32) * r0.astype(F32), axis=1)
     i1 = jnp.sum(t1.astype(F32) * r1.astype(F32), axis=1)
-    input_grad = shuffle(collect(b0, b1, rows))
+    input_grad = shuffle(collect(b0, b1))
     down_part = mm(h0, o0, ((0,), (0,))) + mm(h1, o1, ((0,), (0,)))
     down_part = (down_part * scale).astype(BF)
     down_parts = [down_part[j * dhid : (j + 1) * dhid] for j in range(data_devices)]
@@ -169,13 +178,17 @@
 
     mine = i0.reshape(pairs, rows)
     other = send(i1.reshape(pairs, rows), "expert", 1)
-    both = jnp.stack([mine, other], axis=1)
+    found, source, step = jnp.stack([mine, other], axis=1)[None], [0], 1
+    while step < pairs:
+        half = found.shape[1] // 2
+        got = send(found[:, half:], "expert", 2 * step)
+        found = jnp.concatenate([found[:, :half], got], axis=0)
+        source, step = source + [a ^ step for a in source], 2 * step
     prob_grad = jnp.zeros(expert_ids.shape, F32)
-    for m in range(pairs):
-        got = both[m] if m == 0 else send(both[m], "expert", 2 * m)
+    for at, m in enumerate(source):
         for j in range(2):
             hit = expert_ids == (me ^ (2 * m + j))
-            prob_grad = prob_grad + jnp.where(hit, got[j][:, None], 0.0)
+            prob_grad = prob_grad + jnp.where(hit, found[at, 0, j][:, None], 0.0)
     return (
         mixed,
         input_grad,

time: 164 us -> 144 us (0.88)
  starting transfers between devices: 59.3 us -> 47.1 us
  waiting for transfers between devices: 77.6 us -> 68.9 us
    ppermute x40 -> x37, starting transfers between devices: 59.3 us -> 47.1 us  [send(): return lax.ppermute(x, axis, pairs)]
    ppermute x40 -> x37, waiting for transfers between devices: 77.6 us -> 68.9 us  [send(): return lax.ppermute(x, axis, pairs)]
  transfers between devices with their start and end apart: 40 -> 37, of which waited for: 15 -> 15; matrix products, arithmetic and copies ran while one was open for 13% -> 17% of each run, Pallas kernels for 0% -> 0%
where the time goes in v3:
time: 144 us
  waiting for transfers between devices  68.9 us (48%)
  starting transfers between devices  47.1 us (33%)
  matrix products  14.1 us (10%)
  other arithmetic  10.2 us (7%)
  local copies, waits for them, and re-layouts  2.37 us (2%)
    ppermute x37, waiting for transfers between devices, send(): return lax.ppermute(x, axis, pairs)  68.9 us
    ppermute x37, starting transfers between devices, send(): return lax.ppermute(x, axis, pairs)  47.1 us
    dot_general x18, matrix products, mm(): lax.dot_general(a, b, ((dims[0], dims[1]), ((), ())), preferred_element_t...  14.1 us
  transfers between devices with their start and end apart: 37, of which 15 were waited for; matrix products, arithmetic and copies ran while one was open for 17% of the time, Pallas kernels for 0%

profile of v3, /device:TPU:0, one launch (start us, length us, event | category | flops | bytes accessed | tf_op | source)
XLA Modules:
  0.0 143.9 jit_solution(16749984723398300562)
XLA Ops:
  0.7 0.8 select_reduce_fusion
  1.4 5.1 %collective-permute-start.2 = (f32[8,128]{1,0:T(8,128)S(1)}, f32[8,128]{1,0:T(8,128)S(1)}, u32[]{:S(2)}, u32[]{:S(2)}) collective-permute-start(f32[8,128]{1,0:T(8,128)S(1)} %select_reduce_fusion), channel_id=1, source_target_pairs={{0,6},{1,7},{2,4},{3,5},{4,2},{5,3},{6,0},{7,1},{8,14},{9,15},{10,... | collective-permute-start | bytes 12296 | tf_op jit(solution)/shard_map/ppermute | solution.py:13
  6.5 0.6 collective-permute-start
  7.1 0.7 collective-permute-start.5
  7.8 4.2 %collective-permute-start.3 = (bf16[128,1024]{1,0:T(8,128)(2,1)}, bf16[128,1024]{1,0:T(8,128)(2,1)S(1)}, u32[]{:S(2)}, u32[]{:S(2)}) collective-permute-start(bf16[128,1024]{1,0:T(8,128)(2,1)} %param.7), channel_id=1, source_target_pairs={{0,4},{1,5},{2,6},{3,7},{4,0},{5,1},{6,2},{7,3},{8,12},{9,13},{10,... | collective-permute-start | bytes 786440 | tf_op jit(solution)/shard_map/ppermute | solution.py:13
  12.0 2.0 %pad_maximum_fusion.6 = (bf16[256,1024]{1,0:T(8,128)(2,1)S(1)}, bf16[1024,1024]{1,0:T(8,128)(2,1)}) fusion(bf16[256,512]{1,0:T(8,128)(2,1)} %bitcast.76, bf16[256,512]{1,0:T(8,128)(2,1)} %bitcast.77), kind=kLoop, calls=%fused_computation.44 | loop fusion | flops 1048575 | bytes 1572864 | tf_op jit(solution)/shard_map/concatenate | solution.py:118
  13.9 1.5 %collective-permute-start.11 = (bf16[128,1024]{1,0:T(8,128)(2,1)}, bf16[128,1024]{1,0:T(8,128)(2,1)S(1)}, u32[]{:S(2)}, u32[]{:S(2)}) collective-permute-start(bf16[128,1024]{1,0:T(8,128)(2,1)} %bitcast.78), channel_id=1, source_target_pairs={{0,16},{8,24},{16,0},{24,8},{1,17},{9,25},{17,1},{25,9},{2,18},{10... | collective-permute-start | bytes 786440 | tf_op jit(solution)/shard_map/ppermute | solution.py:13
  15.4 1.5 %collective-permute-start.13 = (bf16[128,1024]{1,0:T(8,128)(2,1)}, bf16[128,1024]{1,0:T(8,128)(2,1)S(1)}, u32[]{:S(2)}, u32[]{:S(2)}) collective-permute-start(bf16[128,1024]{1,0:T(8,128)(2,1)} %bitcast.79), channel_id=1, source_target_pairs={{0,8},{8,0},{16,24},{24,16},{1,9},{9,1},{17,25},{25,17},{2,10},{10... | collective-permute-start | bytes 786440 | tf_op jit(solution)/shard_map/ppermute | solution.py:13
  17.0 4.1 %collective-permute-done.11 = bf16[128,1024]{1,0:T(8,128)(2,1)S(1)} collective-permute-done((bf16[128,1024]{1,0:T(8,128)(2,1)}, bf16[128,1024]{1,0:T(8,128)(2,1)S(1)}, u32[]{:S(2)}, u32[]{:S(2)}) %collective-permute-start.11) | collective-permute-done | bytes 262176 | tf_op jit(solution)/shard_map/ppermute | solution.py:13
  21.4 1.6 %collective-permute-start.12 = (bf16[64,1024]{1,0:T(8,128)(2,1)S(1)}, bf16[64,1024]{1,0:T(8,128)(2,1)S(1)}, u32[]{:S(2)}, u32[]{:S(2)}) collective-permute-start(bf16[64,1024]{1,0:T(8,128)(2,1)S(1)} %slice.231), channel_id=1, source_target_pairs={{0,8},{8,0},{16,24},{24,16},{1,9},{9,1},{17,25},{25,17},{2,10},{10... | collective-permute-start | bytes 393224 | tf_op jit(solution)/shard_map/ppermute | solution.py:13
  23.0 1.6 %collective-permute-start.14 = (bf16[64,1024]{1,0:T(8,128)(2,1)S(1)}, bf16[64,1024]{1,0:T(8,128)(2,1)S(1)}, u32[]{:S(2)}, u32[]{:S(2)}) collective-permute-start(bf16[64,1024]{1,0:T(8,128)(2,1)S(1)} %slice.232), channel_id=1, source_target_pairs={{0,16},{8,24},{16,0},{24,8},{1,17},{9,25},{17,1},{25,9},{2,18},{10... | collective-permute-start | bytes 393224 | tf_op jit(solution)/shard_map/ppermute | solution.py:13
  24.6 2.1 %collective-permute-done.12 = bf16[64,1024]{1,0:T(8,128)(2,1)S(1)} collective-permute-done((bf16[64,1024]{1,0:T(8,128)(2,1)S(1)}, bf16[64,1024]{1,0:T(8,128)(2,1)S(1)}, u32[]{:S(2)}, u32[]{:S(2)}) %collective-permute-start.12) | collective-permute-done | bytes 131104 | tf_op jit(solution)/shard_map/ppermute | solution.py:13
  26.7 1.5 %collective-permute-start.7 = (bf16[256,1024]{1,0:T(8,128)(2,1)S(1)}, bf16[256,1024]{1,0:T(8,128)(2,1)S(1)}, u32[]{:S(2)}, u32[]{:S(2)}) collective-permute-start(bf16[256,1024]{1,0:T(8,128)(2,1)S(1)} %get-tuple-element.55), channel_id=1, source_target_pairs={{0,8},{8,0},{16,24},{24,16},{1,9},{9,1},{17,25},{25,17},{2,10},{10... | collective-permute-start | bytes 1572872 | tf_op jit(solution)/shard_map/ppermute | solution.py:13
  28.2 0.7 collective-permute-done.3
  28.9 2.4 %collective-permute-start.20 = (bf16[128,1024]{1,0:T(8,128)(2,1)S(1)}, bf16[128,1024]{1,0:T(8,128)(2,1)S(1)}, u32[]{:S(2)}, u32[]{:S(2)}) collective-permute-start(bf16[128,1024]{1,0:T(8,128)(2,1)S(1)} %copy-done.2), channel_id=1, source_target_pairs={{0,4},{1,5},{2,6},{3,7},{4,0},{5,1},{6,2},{7,3},{8,12},{9,13},{10,... | collective-permute-start | bytes 786440 | tf_op jit(solution)/shard_map/ppermute | solution.py:13
  31.3 1.3 collective-permute-start.6
  32.8 1.6 %collective-permute-start.8 = (bf16[256,1024]{1,0:T(8,128)(2,1)S(1)}, bf16[256,1024]{1,0:T(8,128)(2,1)S(1)}, u32[]{:S(2)}, u32[]{:S(2)}) collective-permute-start(bf16[256,1024]{1,0:T(8,128)(2,1)S(1)} %get-tuple-element.55), channel_id=1, source_target_pairs={{0,16},{8,24},{16,0},{24,8},{1,17},{9,25},{17,1},{25,9},{2,18},{10... | collective-permute-start | bytes 1572872 | tf_op jit(solution)/shard_map/ppermute | solution.py:13
  34.4 9.9 %collective-permute-done.6 = bf16[128,1024]{1,0:T(8,128)(2,1)S(1)} collective-permute-done((bf16[128,1024]{1,0:T(8,128)(2,1)S(1)}, bf16[128,1024]{1,0:T(8,128)(2,1)S(1)}, u32[]{:S(2)}, u32[]{:S(2)}) %collective-permute-start.6) | collective-permute-done | bytes 262176 | tf_op jit(solution)/shard_map/ppermute | solution.py:13
  44.4 0.7 collective-permute-start.22
  45.1 2.1 %collective-permute-start.21 = (bf16[128,1024]{1,0:T(8,128)(2,1)S(1)}, bf16[128,1024]{1,0:T(8,128)(2,1)S(1)}, u32[]{:S(2)}, u32[]{:S(2)}) collective-permute-start(bf16[128,1024]{1,0:T(8,128)(2,1)S(1)} %copy-done.2), channel_id=1, source_target_pairs={{0,2},{1,3},{2,0},{3,1},{4,6},{5,7},{6,4},{7,5},{8,10},{9,11},{10,... | collective-permute-start | bytes 786440 | tf_op jit(solution)/shard_map/ppermute | solution.py:13
  47.2 1.3 collective-permute-start.23
  49.0 1.6 %collective-permute-start.9 = (bf16[128,1024]{1,0:T(8,128)(2,1)S(1)}, bf16[128,1024]{1,0:T(8,128)(2,1)S(1)}, u32[]{:S(2)}, u32[]{:S(2)}) collective-permute-start(bf16[128,1024]{1,0:T(8,128)(2,1)S(1)} %slice.227), channel_id=1, source_target_pairs={{0,8},{8,0},{16,24},{24,16},{1,9},{9,1},{17,25},{25,17},{2,10},{10... | collective-permute-start | bytes 786440 | tf_op jit(solution)/shard_map/ppermute | solution.py:13
  50.6 1.6 %collective-permute-start.10 = (bf16[128,1024]{1,0:T(8,128)(2,1)S(1)}, bf16[128,1024]{1,0:T(8,128)(2,1)S(1)}, u32[]{:S(2)}, u32[]{:S(2)}) collective-permute-start(bf16[128,1024]{1,0:T(8,128)(2,1)S(1)} %slice.228), channel_id=1, source_target_pairs={{0,16},{8,24},{16,0},{24,8},{1,17},{9,25},{17,1},{25,9},{2,18},{10... | collective-permute-start | bytes 786440 | tf_op jit(solution)/shard_map/ppermute | solution.py:13
  52.1 6.0 %collective-permute-done.23 = bf16[128,1024]{1,0:T(8,128)(2,1)S(1)} collective-permute-done((bf16[128,1024]{1,0:T(8,128)(2,1)S(1)}, bf16[128,1024]{1,0:T(8,128)(2,1)S(1)}, u32[]{:S(2)}, u32[]{:S(2)}) %collective-permute-start.23) | collective-permute-done | bytes 262176 | tf_op jit(solution)/shard_map/ppermute | solution.py:13
  58.6 1.2 copy-done.3
  59.9 1.3 fusion.24
  61.5 0.7 convolution_convert_fusion.3
  62.3 1.3 fusion.25
  63.9 0.7 multiply_convert_fusion.3
  64.6 1.0 multiply_convert_fusion.8
  65.8 0.5 fusion.12
  67.3 0.5 fusion.21
  67.8 1.3 convolution_convert_fusion.1
  69.3 1.0 multiply_convert_fusion.6
  70.5 1.3 convolution_convert_fusion
  71.8 0.6 collective-permute-start.25
  73.7 0.7 fusion.5
  74.9 0.7 fusion.26
  75.6 0.7 multiply_convert_fusion
  76.4 2.5 %collective-permute-start.36 = (bf16[128,1024]{1,0:T(8,128)(2,1)S(1)}, bf16[128,1024]{1,0:T(8,128)(2,1)S(1)}, u32[]{:S(2)}, u32[]{:S(2)}) collective-permute-start(bf16[128,1024]{1,0:T(8,128)(2,1)S(1)} %get-tuple-element.44), channel_id=1, source_target_pairs={{0,24},{8,16},{16,8},{24,0},{1,25},{9,17},{17,9},{25,1},{2,26},{10... | collective-permute-start | bytes 786440 | tf_op jit(solution)/shard_map/ppermute | solution.py:13
  79.0 0.5 collective-permute-start.35
  79.9 0.9 collective-permute-start.29
  80.7 2.8 %collective-permute-done.29 = f32[1,2,2,128]{3,2,1,0:T(2,128)S(1)} collective-permute-done((f32[1,2,2,128]{3,2,1,0:T(2,128)S(1)}, f32[1,2,2,128]{3,2,1,0:T(2,128)S(1)}, u32[]{:S(2)}, u32[]{:S(2)}) %collective-permute-start.29) | collective-permute-done | bytes 2080 | tf_op jit(solution)/shard_map/ppermute | solution.py:13
  83.5 1.0 collective-permute-start.30
  84.5 3.5 %collective-permute-done.30 = f32[2,1,2,128]{3,2,1,0:T(2,128)S(1)} collective-permute-done((f32[2,1,2,128]{3,2,1,0:T(2,128)S(1)}, f32[2,1,2,128]{3,2,1,0:T(2,128)S(1)}, u32[]{:S(2)}, u32[]{:S(2)}) %collective-permute-start.30) | collective-permute-done | bytes 2080 | tf_op jit(solution)/shard_map/ppermute | solution.py:13
  88.0 0.5 collective-permute-start.34
  88.5 0.6 select_add_fusion
  89.1 2.5 %collective-permute-start.33 = (bf16[256,1024]{1,0:T(8,128)(2,1)S(1)}, bf16[256,1024]{1,0:T(8,128)(2,1)S(1)}, u32[]{:S(2)}, u32[]{:S(2)}) collective-permute-start(bf16[256,1024]{1,0:T(8,128)(2,1)S(1)} %fusion.7), channel_id=1, source_target_pairs={{0,24},{8,16},{16,8},{24,0},{1,25},{9,17},{17,9},{25,1},{2,26},{10... | collective-permute-start | bytes 1572872 | tf_op jit(solution)/shard_map/ppermute | solution.py:13
  91.7 1.6 %collective-permute-start.32 = (bf16[256,1024]{1,0:T(8,128)(2,1)S(1)}, bf16[256,1024]{1,0:T(8,128)(2,1)S(1)}, u32[]{:S(2)}, u32[]{:S(2)}) collective-permute-start(bf16[256,1024]{1,0:T(8,128)(2,1)S(1)} %fusion.6), channel_id=1, source_target_pairs={{0,16},{8,24},{16,0},{24,8},{1,17},{9,25},{17,1},{25,9},{2,18},{10... | collective-permute-start | bytes 1572872 | tf_op jit(solution)/shard_map/ppermute | solution.py:13
  93.4 3.8 %collective-permute-done.34 = bf16[128,1024]{1,0:T(8,128)(2,1)S(1)} collective-permute-done((bf16[128,1024]{1,0:T(8,128)(2,1)S(1)}, bf16[128,1024]{1,0:T(8,128)(2,1)S(1)}, u32[]{:S(2)}, u32[]{:S(2)}) %collective-permute-start.34) | collective-permute-done | bytes 262176 | tf_op jit(solution)/shard_map/ppermute | solution.py:13
  97.2 0.5 collective-permute-start.31
  97.7 1.0 fusion.10
  99.1 1.8 %collective-permute-start.18 = (bf16[256,1024]{1,0:T(8,128)(2,1)S(1)}, bf16[256,1024]{1,0:T(8,128)(2,1)S(1)}, u32[]{:S(2)}, u32[]{:S(2)}) collective-permute-start(bf16[256,1024]{1,0:T(8,128)(2,1)S(1)} %slice.236), channel_id=1, source_target_pairs={{0,2},{1,3},{2,0},{3,1},{4,6},{5,7},{6,4},{7,5},{8,10},{9,11},{10,... | collective-permute-start | bytes 1572872 | tf_op jit(solution)/shard_map/ppermute | solution.py:13
  101.8 7.6 %collective-permute-done.33 = bf16[256,1024]{1,0:T(8,128)(2,1)S(1)} collective-permute-done((bf16[256,1024]{1,0:T(8,128)(2,1)S(1)}, bf16[256,1024]{1,0:T(8,128)(2,1)S(1)}, u32[]{:S(2)}, u32[]{:S(2)}) %collective-permute-start.33) | collective-permute-done | bytes 524320 | tf_op jit(solution)/shard_map/ppermute | solution.py:13
  109.4 6.6 %collective-permute-done.32 = bf16[256,1024]{1,0:T(8,128)(2,1)S(1)} collective-permute-done((bf16[256,1024]{1,0:T(8,128)(2,1)S(1)}, bf16[256,1024]{1,0:T(8,128)(2,1)S(1)}, u32[]{:S(2)}, u32[]{:S(2)}) %collective-permute-start.32) | collective-permute-done | bytes 524320 | tf_op jit(solution)/shard_map/ppermute | solution.py:13
  116.0 1.0 collective-permute-done.31
  117.3 0.8 slice_bitcast_fusion
  118.1 1.8 %collective-permute-done.26 = bf16[256,1024]{1,0:T(8,128)(2,1)S(1)} collective-permute-done((bf16[256,1024]{1,0:T(8,128)(2,1)S(1)}, bf16[256,1024]{1,0:T(8,128)(2,1)S(1)}, u32[]{:S(2)}, u32[]{:S(2)}) %collective-permute-start.26) | collective-permute-done | bytes 524320 | tf_op jit(solution)/shard_map/ppermute | solution.py:13
  120.2 2.4 %collective-permute-start.27 = (bf16[128,1024]{1,0:T(8,128)(2,1)S(1)}, bf16[128,1024]{1,0:T(8,128)(2,1)S(1)}, u32[]{:S(2)}, u32[]{:S(2)}) collective-permute-start(bf16[128,1024]{1,0:T(8,128)(2,1)S(1)} %slice.242), channel_id=1, source_target_pairs={{0,4},{1,5},{2,6},{3,7},{4,0},{5,1},{6,2},{7,3},{8,12},{9,13},{10,... | collective-permute-start | bytes 786440 | tf_op jit(solution)/shard_map/ppermute | solution.py:13
  122.8 0.7 collective-permute-start.19
  123.4 15.0 %collective-permute-done.27 = bf16[128,1024]{1,0:T(8,128)(2,1)S(1)} collective-permute-done((bf16[128,1024]{1,0:T(8,128)(2,1)S(1)}, bf16[128,1024]{1,0:T(8,128)(2,1)S(1)}, u32[]{:S(2)}, u32[]{:S(2)}) %collective-permute-start.27) | collective-permute-done | bytes 262176 | tf_op jit(solution)/shard_map/ppermute | solution.py:13
  138.6 0.7 pad_maximum_fusion.7
  139.3 3.8 %collective-permute-done.19 = bf16[128,1024]{1,0:T(8,128)(2,1)S(1)} collective-permute-done((bf16[128,1024]{1,0:T(8,128)(2,1)S(1)}, bf16[128,1024]{1,0:T(8,128)(2,1)S(1)}, u32[]{:S(2)}, u32[]{:S(2)}) %collective-permute-start.19) | collective-permute-done | bytes 262176 | tf_op jit(solution)/shard_map/ppermute | solution.py:13
  143.1 0.8 add_convert_fusion.7
  (94 shorter events, 8.2 us)
Async XLA Ops:
  0.6 32.0 %copy-start = (bf16[1,128,1024]{2,1,0:T(8,128)(2,1)S(1)}, bf16[1,128,1024]{2,1,0:T(8,128)(2,1)}, u32[]{:S(2)}) copy-start(bf16[1,128,1024]{2,1,0:T(8,128)(2,1)} %param.12) | copy-start | bytes 786436
  0.6 28.3 %copy-start.2 = (bf16[128,1024]{1,0:T(8,128)(2,1)S(1)}, bf16[128,1024]{1,0:T(8,128)(2,1)}, u32[]{:S(2)}) copy-start(bf16[128,1024]{1,0:T(8,128)(2,1)} %param.13) | copy-start | bytes 786436
  1.4 12.5 %collective-permute-start.2 = (f32[8,128]{1,0:T(8,128)S(1)}, f32[8,128]{1,0:T(8,128)S(1)}, u32[]{:S(2)}, u32[]{:S(2)}) collective-permute-start(f32[8,128]{1,0:T(8,128)S(1)} %select_reduce_fusion), channel_id=1, source_target_pairs={{0,6},{1,7},{2,4},{3,5},{4,2},{5,3},{6,0},{7,1},{8,14},{9,15},{10,... | collective-permute-start | bytes 12296 | tf_op jit(solution)/shard_map/ppermute | solution.py:13
  6.5 8.9 %collective-permute-start.1 = (f32[8,128]{1,0:T(8,128)S(1)}, f32[8,128]{1,0:T(8,128)S(1)}, u32[]{:S(2)}, u32[]{:S(2)}) collective-permute-start(f32[8,128]{1,0:T(8,128)S(1)} %select_reduce_fusion), channel_id=1, source_target_pairs={{0,2},{1,3},{2,0},{3,1},{4,6},{5,7},{6,4},{7,5},{8,10},{9,11},{10,... | collective-permute-start | bytes 12296 | tf_op jit(solution)/shard_map/ppermute | solution.py:13
  6.5 10.4 %collective-permute-start = (f32[8,128]{1,0:T(8,128)S(1)}, f32[8,128]{1,0:T(8,128)S(1)}, u32[]{:S(2)}, u32[]{:S(2)}) collective-permute-start(f32[8,128]{1,0:T(8,128)S(1)} %select_reduce_fusion), channel_id=1, source_target_pairs={{0,4},{1,5},{2,6},{3,7},{4,0},{5,1},{6,2},{7,3},{8,12},{9,13},{10,... | collective-permute-start | bytes 12296 | tf_op jit(solution)/shard_map/ppermute | solution.py:13
  7.1 25.7 %collective-permute-start.5 = (bf16[128,1024]{1,0:T(8,128)(2,1)}, bf16[128,1024]{1,0:T(8,128)(2,1)S(1)}, u32[]{:S(2)}, u32[]{:S(2)}) collective-permute-start(bf16[128,1024]{1,0:T(8,128)(2,1)} %param.7), channel_id=1, source_target_pairs={{2,4},{3,5},{4,2},{5,3},{10,12},{11,13},{12,10},{13,11},{18,20},{1... | collective-permute-start | bytes 786440 | tf_op jit(solution)/shard_map/ppermute | solution.py:13
  7.8 21.1 %collective-permute-start.3 = (bf16[128,1024]{1,0:T(8,128)(2,1)}, bf16[128,1024]{1,0:T(8,128)(2,1)S(1)}, u32[]{:S(2)}, u32[]{:S(2)}) collective-permute-start(bf16[128,1024]{1,0:T(8,128)(2,1)} %param.7), channel_id=1, source_target_pairs={{0,4},{1,5},{2,6},{3,7},{4,0},{5,1},{6,2},{7,3},{8,12},{9,13},{10,... | collective-permute-start | bytes 786440 | tf_op jit(solution)/shard_map/ppermute | solution.py:13
  13.9 7.1 %collective-permute-start.11 = (bf16[128,1024]{1,0:T(8,128)(2,1)}, bf16[128,1024]{1,0:T(8,128)(2,1)S(1)}, u32[]{:S(2)}, u32[]{:S(2)}) collective-permute-start(bf16[128,1024]{1,0:T(8,128)(2,1)} %bitcast.78), channel_id=1, source_target_pairs={{0,16},{8,24},{16,0},{24,8},{1,17},{9,25},{17,1},{25,9},{2,18},{10... | collective-permute-start | bytes 786440 | tf_op jit(solution)/shard_map/ppermute | solution.py:13
  15.4 7.5 %collective-permute-start.13 = (bf16[128,1024]{1,0:T(8,128)(2,1)}, bf16[128,1024]{1,0:T(8,128)(2,1)S(1)}, u32[]{:S(2)}, u32[]{:S(2)}) collective-permute-start(bf16[128,1024]{1,0:T(8,128)(2,1)} %bitcast.79), channel_id=1, source_target_pairs={{0,8},{8,0},{16,24},{24,16},{1,9},{9,1},{17,25},{25,17},{2,10},{10... | collective-permute-start | bytes 786440 | tf_op jit(solution)/shard_map/ppermute | solution.py:13
  16.9 4.4 %collective-permute-start.15 = (f32[4,8,128]{2,1,0:T(8,128)S(1)}, f32[4,8,128]{2,1,0:T(8,128)S(1)}, u32[]{:S(2)}, u32[]{:S(2)}) collective-permute-start(f32[4,8,128]{2,1,0:T(8,128)S(1)} %pad_maximum_fusion.8), channel_id=1, source_target_pairs={{0,1},{1,0},{2,3},{3,2},{4,5},{5,4},{6,7},{7,6},{8,9},{9,8},{10,11... | collective-permute-start | bytes 49160 | tf_op jit(solution)/shard_map/ppermute | solution.py:13
  21.1 24.0 %collective-permute-start.4 = (bf16[128,1024]{1,0:T(8,128)(2,1)}, bf16[128,1024]{1,0:T(8,128)(2,1)S(1)}, u32[]{:S(2)}, u32[]{:S(2)}) collective-permute-start(bf16[128,1024]{1,0:T(8,128)(2,1)} %param.7), channel_id=1, source_target_pairs={{0,2},{1,3},{2,0},{3,1},{4,6},{5,7},{6,4},{7,5},{8,10},{9,11},{10,... | collective-permute-start | bytes 786440 | tf_op jit(solution)/shard_map/ppermute | solution.py:13
  21.4 5.3 %collective-permute-start.12 = (bf16[64,1024]{1,0:T(8,128)(2,1)S(1)}, bf16[64,1024]{1,0:T(8,128)(2,1)S(1)}, u32[]{:S(2)}, u32[]{:S(2)}) collective-permute-start(bf16[64,1024]{1,0:T(8,128)(2,1)S(1)} %slice.231), channel_id=1, source_target_pairs={{0,8},{8,0},{16,24},{24,16},{1,9},{9,1},{17,25},{25,17},{2,10},{10... | collective-permute-start | bytes 393224 | tf_op jit(solution)/shard_map/ppermute | solution.py:13
  23.0 8.3 %collective-permute-start.14 = (bf16[64,1024]{1,0:T(8,128)(2,1)S(1)}, bf16[64,1024]{1,0:T(8,128)(2,1)S(1)}, u32[]{:S(2)}, u32[]{:S(2)}) collective-permute-start(bf16[64,1024]{1,0:T(8,128)(2,1)S(1)} %slice.232), channel_id=1, source_target_pairs={{0,16},{8,24},{16,0},{24,8},{1,17},{9,25},{17,1},{25,9},{2,18},{10... | collective-permute-start | bytes 393224 | tf_op jit(solution)/shard_map/ppermute | solution.py:13
  26.7 22.2 %collective-permute-start.7 = (bf16[256,1024]{1,0:T(8,128)(2,1)S(1)}, bf16[256,1024]{1,0:T(8,128)(2,1)S(1)}, u32[]{:S(2)}, u32[]{:S(2)}) collective-permute-start(bf16[256,1024]{1,0:T(8,128)(2,1)S(1)} %get-tuple-element.55), channel_id=1, source_target_pairs={{0,8},{8,0},{16,24},{24,16},{1,9},{9,1},{17,25},{25,17},{2,10},{10... | collective-permute-start | bytes 1572872 | tf_op jit(solution)/shard_map/ppermute | solution.py:13
  28.9 18.3 %collective-permute-start.20 = (bf16[128,1024]{1,0:T(8,128)(2,1)S(1)}, bf16[128,1024]{1,0:T(8,128)(2,1)S(1)}, u32[]{:S(2)}, u32[]{:S(2)}) collective-permute-start(bf16[128,1024]{1,0:T(8,128)(2,1)S(1)} %copy-done.2), channel_id=1, source_target_pairs={{0,4},{1,5},{2,6},{3,7},{4,0},{5,1},{6,2},{7,3},{8,12},{9,13},{10,... | collective-permute-start | bytes 786440 | tf_op jit(solution)/shard_map/ppermute | solution.py:13
  31.3 13.0 %collective-permute-start.6 = (bf16[128,1024]{1,0:T(8,128)(2,1)S(1)}, bf16[128,1024]{1,0:T(8,128)(2,1)S(1)}, u32[]{:S(2)}, u32[]{:S(2)}) collective-permute-start(bf16[128,1024]{1,0:T(8,128)(2,1)S(1)} %collective-permute-done.3), channel_id=1, source_target_pairs={{2,0},{3,1},{4,6},{5,7},{10,8},{11,9},{12,14},{13,15},{18,16},{19,... | collective-permute-start | bytes 786440 | tf_op jit(solution)/shard_map/ppermute | solution.py:13
  32.6 15.9 %copy-start.1 = (bf16[128,1024]{1,0:T(8,128)(2,1)S(1)}, bf16[128,1024]{1,0:T(8,128)(2,1)}, u32[]{:S(2)}) copy-start(bf16[128,1024]{1,0:T(8,128)(2,1)} %param.7) | copy-start | bytes 786436
  32.8 16.0 %collective-permute-start.8 = (bf16[256,1024]{1,0:T(8,128)(2,1)S(1)}, bf16[256,1024]{1,0:T(8,128)(2,1)S(1)}, u32[]{:S(2)}, u32[]{:S(2)}) collective-permute-start(bf16[256,1024]{1,0:T(8,128)(2,1)S(1)} %get-tuple-element.55), channel_id=1, source_target_pairs={{0,16},{8,24},{16,0},{24,8},{1,17},{9,25},{17,1},{25,9},{2,18},{10... | collective-permute-start | bytes 1572872 | tf_op jit(solution)/shard_map/ppermute | solution.py:13
  44.4 6.2 %collective-permute-start.22 = (bf16[128,1024]{1,0:T(8,128)(2,1)S(1)}, bf16[128,1024]{1,0:T(8,128)(2,1)S(1)}, u32[]{:S(2)}, u32[]{:S(2)}) collective-permute-start(bf16[128,1024]{1,0:T(8,128)(2,1)S(1)} %copy-done.2), channel_id=1, source_target_pairs={{2,4},{3,5},{4,2},{5,3},{10,12},{11,13},{12,10},{13,11},{18,20},{1... | collective-permute-start | bytes 786440 | tf_op jit(solution)/shard_map/ppermute | solution.py:13
  45.1 13.1 %collective-permute-start.21 = (bf16[128,1024]{1,0:T(8,128)(2,1)S(1)}, bf16[128,1024]{1,0:T(8,128)(2,1)S(1)}, u32[]{:S(2)}, u32[]{:S(2)}) collective-permute-start(bf16[128,1024]{1,0:T(8,128)(2,1)S(1)} %copy-done.2), channel_id=1, source_target_pairs={{0,2},{1,3},{2,0},{3,1},{4,6},{5,7},{6,4},{7,5},{8,10},{9,11},{10,... | collective-permute-start | bytes 786440 | tf_op jit(solution)/shard_map/ppermute | solution.py:13
  47.2 10.9 %collective-permute-start.23 = (bf16[128,1024]{1,0:T(8,128)(2,1)S(1)}, bf16[128,1024]{1,0:T(8,128)(2,1)S(1)}, u32[]{:S(2)}, u32[]{:S(2)}) collective-permute-start(bf16[128,1024]{1,0:T(8,128)(2,1)S(1)} %collective-permute-done.20), channel_id=1, source_target_pairs={{2,0},{3,1},{4,6},{5,7},{10,8},{11,9},{12,14},{13,15},{18,16},{19,... | collective-permute-start | bytes 786440 | tf_op jit(solution)/shard_map/ppermute | solution.py:13
  48.8 13.4 %collective-permute-start.16 = (bf16[512,1024]{1,0:T(8,128)(2,1)S(1)}, bf16[512,1024]{1,0:T(8,128)(2,1)S(1)}, u32[]{:S(2)}, u32[]{:S(2)}) collective-permute-start(bf16[512,1024]{1,0:T(8,128)(2,1)S(1)} %pad_maximum_fusion.1), channel_id=1, source_target_pairs={{0,1},{1,0},{2,3},{3,2},{4,5},{5,4},{6,7},{7,6},{8,9},{9,8},{10,11... | collective-permute-start | bytes 3145736 | tf_op jit(solution)/shard_map/ppermute | solution.py:13
  49.0 10.9 %collective-permute-start.9 = (bf16[128,1024]{1,0:T(8,128)(2,1)S(1)}, bf16[128,1024]{1,0:T(8,128)(2,1)S(1)}, u32[]{:S(2)}, u32[]{:S(2)}) collective-permute-start(bf16[128,1024]{1,0:T(8,128)(2,1)S(1)} %slice.227), channel_id=1, source_target_pairs={{0,8},{8,0},{16,24},{24,16},{1,9},{9,1},{17,25},{25,17},{2,10},{10... | collective-permute-start | bytes 786440 | tf_op jit(solution)/shard_map/ppermute | solution.py:13
  50.6 9.3 %collective-permute-start.10 = (bf16[128,1024]{1,0:T(8,128)(2,1)S(1)}, bf16[128,1024]{1,0:T(8,128)(2,1)S(1)}, u32[]{:S(2)}, u32[]{:S(2)}) collective-permute-start(bf16[128,1024]{1,0:T(8,128)(2,1)S(1)} %slice.228), channel_id=1, source_target_pairs={{0,16},{8,24},{16,0},{24,8},{1,17},{9,25},{17,1},{25,9},{2,18},{10... | collective-permute-start | bytes 786440 | tf_op jit(solution)/shard_map/ppermute | solution.py:13
  58.2 1.6 %copy-start.3 = (bf16[1024,1024]{1,0:T(8,128)(2,1)S(1)}, bf16[1024,1024]{1,0:T(8,128)(2,1)}, u32[]{:S(2)}) copy-start(bf16[1024,1024]{1,0:T(8,128)(2,1)} %get-tuple-element.56) | copy-start | bytes 6291460
  58.3 10.8 %collective-permute-start.24 = (bf16[512,1024]{1,0:T(8,128)(2,1)S(1)}, bf16[512,1024]{1,0:T(8,128)(2,1)S(1)}, u32[]{:S(2)}, u32[]{:S(2)}) collective-permute-start(bf16[512,1024]{1,0:T(8,128)(2,1)S(1)} %pad_maximum_fusion.3), channel_id=1, source_target_pairs={{0,1},{1,0},{2,3},{3,2},{4,5},{5,4},{6,7},{7,6},{8,9},{9,8},{10,11... | collective-permute-start | bytes 3145736 | tf_op jit(solution)/shard_map/ppermute | solution.py:13
  66.7 32.0 %collective-permute-start.17 = (bf16[512,1024]{1,0:T(8,128)(2,1)S(1)}, bf16[512,1024]{1,0:T(8,128)(2,1)S(1)}, u32[]{:S(2)}, u32[]{:S(2)}) collective-permute-start(bf16[512,1024]{1,0:T(8,128)(2,1)S(1)} %get-tuple-element.71), channel_id=1, source_target_pairs={{0,1},{1,0},{2,3},{3,2},{4,5},{5,4},{6,7},{7,6},{8,9},{9,8},{10,11... | collective-permute-start | bytes 3145736 | tf_op jit(solution)/shard_map/ppermute | solution.py:13
  71.8 29.2 %collective-permute-start.25 = (bf16[512,1024]{1,0:T(8,128)(2,1)S(1)}, bf16[512,1024]{1,0:T(8,128)(2,1)S(1)}, u32[]{:S(2)}, u32[]{:S(2)}) collective-permute-start(bf16[512,1024]{1,0:T(8,128)(2,1)S(1)} %convolution_convert_fusion), channel_id=1, source_target_pairs={{0,1},{1,0},{2,3},{3,2},{4,5},{5,4},{6,7},{7,6},{8,9},{9,8},{10,11... | collective-permute-start | bytes 3145736 | tf_op jit(solution)/shard_map/ppermute | solution.py:13
  72.7 7.1 %collective-permute-start.28 = (f32[4,128]{1,0:T(4,128)S(1)}, f32[4,128]{1,0:T(4,128)S(1)}, u32[]{:S(2)}, u32[]{:S(2)}) collective-permute-start(f32[4,128]{1,0:T(4,128)S(1)} %bitcast.90), channel_id=1, source_target_pairs={{0,1},{1,0},{2,3},{3,2},{4,5},{5,4},{6,7},{7,6},{8,9},{9,8},{10,11... | collective-permute-start | bytes 6152 | tf_op jit(solution)/shard_map/ppermute | solution.py:13
  76.4 12.2 %copy-start.4 = (s32[128,4]{0,1:T(4,128)S(1)}, s32[128,4]{0,1:T(4,128)}, u32[]{:S(2)}) copy-start(s32[128,4]{0,1:T(4,128)} %param.8) | copy-start | bytes 6148
  76.4 12.7 %collective-permute-start.36 = (bf16[128,1024]{1,0:T(8,128)(2,1)S(1)}, bf16[128,1024]{1,0:T(8,128)(2,1)S(1)}, u32[]{:S(2)}, u32[]{:S(2)}) collective-permute-start(bf16[128,1024]{1,0:T(8,128)(2,1)S(1)} %get-tuple-element.44), channel_id=1, source_target_pairs={{0,24},{8,16},{16,8},{24,0},{1,25},{9,17},{17,9},{25,1},{2,26},{10... | collective-permute-start | bytes 786440 | tf_op jit(solution)/shard_map/ppermute | solution.py:13
  79.0 12.8 %collective-permute-start.35 = (bf16[128,1024]{1,0:T(8,128)(2,1)S(1)}, bf16[128,1024]{1,0:T(8,128)(2,1)S(1)}, u32[]{:S(2)}, u32[]{:S(2)}) collective-permute-start(bf16[128,1024]{1,0:T(8,128)(2,1)S(1)} %get-tuple-element.43), channel_id=1, source_target_pairs={{0,16},{8,24},{16,0},{24,8},{1,17},{9,25},{17,1},{25,9},{2,18},{10... | collective-permute-start | bytes 786440 | tf_op jit(solution)/shard_map/ppermute | solution.py:13
  79.9 3.7 %collective-permute-start.29 = (f32[1,2,2,128]{3,2,1,0:T(2,128)S(1)}, f32[1,2,2,128]{3,2,1,0:T(2,128)S(1)}, u32[]{:S(2)}, u32[]{:S(2)}) collective-permute-start(f32[1,2,2,128]{3,2,1,0:T(2,128)S(1)} %get-tuple-element.64), channel_id=1, source_target_pairs={{0,2},{1,3},{2,0},{3,1},{4,6},{5,7},{6,4},{7,5},{8,10},{9,11},{10,... | collective-permute-start | bytes 6152 | tf_op jit(solution)/shard_map/ppermute | solution.py:13
  83.5 4.5 %collective-permute-start.30 = (f32[2,1,2,128]{3,2,1,0:T(2,128)S(1)}, f32[2,1,2,128]{3,2,1,0:T(2,128)S(1)}, u32[]{:S(2)}, u32[]{:S(2)}) collective-permute-start(f32[2,1,2,128]{3,2,1,0:T(2,128)S(1)} %pad_maximum_fusion.9), channel_id=1, source_target_pairs={{0,4},{1,5},{2,6},{3,7},{4,0},{5,1},{6,2},{7,3},{8,12},{9,13},{10,... | collective-permute-start | bytes 6152 | tf_op jit(solution)/shard_map/ppermute | solution.py:13
  88.0 9.2 %collective-permute-start.34 = (bf16[128,1024]{1,0:T(8,128)(2,1)S(1)}, bf16[128,1024]{1,0:T(8,128)(2,1)S(1)}, u32[]{:S(2)}, u32[]{:S(2)}) collective-permute-start(bf16[128,1024]{1,0:T(8,128)(2,1)S(1)} %get-tuple-element.42), channel_id=1, source_target_pairs={{0,8},{8,0},{16,24},{24,16},{1,9},{9,1},{17,25},{25,17},{2,10},{10... | collective-permute-start | bytes 786440 | tf_op jit(solution)/shard_map/ppermute | solution.py:13
  89.1 20.3 %collective-permute-start.33 = (bf16[256,1024]{1,0:T(8,128)(2,1)S(1)}, bf16[256,1024]{1,0:T(8,128)(2,1)S(1)}, u32[]{:S(2)}, u32[]{:S(2)}) collective-permute-start(bf16[256,1024]{1,0:T(8,128)(2,1)S(1)} %fusion.7), channel_id=1, source_target_pairs={{0,24},{8,16},{16,8},{24,0},{1,25},{9,17},{17,9},{25,1},{2,26},{10... | collective-permute-start | bytes 1572872 | tf_op jit(solution)/shard_map/ppermute | solution.py:13
  91.7 24.2 %collective-permute-start.32 = (bf16[256,1024]{1,0:T(8,128)(2,1)S(1)}, bf16[256,1024]{1,0:T(8,128)(2,1)S(1)}, u32[]{:S(2)}, u32[]{:S(2)}) collective-permute-start(bf16[256,1024]{1,0:T(8,128)(2,1)S(1)} %fusion.6), channel_id=1, source_target_pairs={{0,16},{8,24},{16,0},{24,8},{1,17},{9,25},{17,1},{25,9},{2,18},{10... | collective-permute-start | bytes 1572872 | tf_op jit(solution)/shard_map/ppermute | solution.py:13
  97.2 19.8 %collective-permute-start.31 = (bf16[256,1024]{1,0:T(8,128)(2,1)S(1)}, bf16[256,1024]{1,0:T(8,128)(2,1)S(1)}, u32[]{:S(2)}, u32[]{:S(2)}) collective-permute-start(bf16[256,1024]{1,0:T(8,128)(2,1)S(1)} %fusion.5), channel_id=1, source_target_pairs={{0,8},{8,0},{16,24},{24,16},{1,9},{9,1},{17,25},{25,17},{2,10},{10... | collective-permute-start | bytes 1572872 | tf_op jit(solution)/shard_map/ppermute | solution.py:13
  99.1 23.4 %collective-permute-start.18 = (bf16[256,1024]{1,0:T(8,128)(2,1)S(1)}, bf16[256,1024]{1,0:T(8,128)(2,1)S(1)}, u32[]{:S(2)}, u32[]{:S(2)}) collective-permute-start(bf16[256,1024]{1,0:T(8,128)(2,1)S(1)} %slice.236), channel_id=1, source_target_pairs={{0,2},{1,3},{2,0},{3,1},{4,6},{5,7},{6,4},{7,5},{8,10},{9,11},{10,... | collective-permute-start | bytes 1572872 | tf_op jit(solution)/shard_map/ppermute | solution.py:13
  101.4 18.5 %collective-permute-start.26 = (bf16[256,1024]{1,0:T(8,128)(2,1)S(1)}, bf16[256,1024]{1,0:T(8,128)(2,1)S(1)}, u32[]{:S(2)}, u32[]{:S(2)}) collective-permute-start(bf16[256,1024]{1,0:T(8,128)(2,1)S(1)} %slice.240), channel_id=1, source_target_pairs={{0,2},{1,3},{2,0},{3,1},{4,6},{5,7},{6,4},{7,5},{8,10},{9,11},{10,... | collective-permute-start | bytes 1572872 | tf_op jit(solution)/shard_map/ppermute | solution.py:13
  120.2 18.3 %collective-permute-start.27 = (bf16[128,1024]{1,0:T(8,128)(2,1)S(1)}, bf16[128,1024]{1,0:T(8,128)(2,1)S(1)}, u32[]{:S(2)}, u32[]{:S(2)}) collective-permute-start(bf16[128,1024]{1,0:T(8,128)(2,1)S(1)} %slice.242), channel_id=1, source_target_pairs={{0,4},{1,5},{2,6},{3,7},{4,0},{5,1},{6,2},{7,3},{8,12},{9,13},{10,... | collective-permute-start | bytes 786440 | tf_op jit(solution)/shard_map/ppermute | solution.py:13
  122.8 20.3 %collective-permute-start.19 = (bf16[128,1024]{1,0:T(8,128)(2,1)S(1)}, bf16[128,1024]{1,0:T(8,128)(2,1)S(1)}, u32[]{:S(2)}, u32[]{:S(2)}) collective-permute-start(bf16[128,1024]{1,0:T(8,128)(2,1)S(1)} %slice.238), channel_id=1, source_target_pairs={{0,4},{1,5},{2,6},{3,7},{4,0},{5,1},{6,2},{7,3},{8,12},{9,13},{10,... | collective-permute-start | bytes 786440 | tf_op jit(solution)/shard_map/ppermute | solution.py:13
